TPU v7x, 256 devices: a whole 4x4x8 slice. The times are simulated.
256 devices in a mesh: tile: 128 (over z, x_lo, y, core), ch: 2 (over x_hi).
Axes of the slice: x: 4 (x_hi: 2, x_lo: 2; x = x_hi * 2 + x_lo), y: 4, z: 8, core: 2. Of those that a mesh axis runs over, the one named last changes fastest.
Arguments:
- features: bfloat16 [128, 32, 32, 384], P('tile', None, None, 'ch'), may hold values from -6 to 6
- weight: bfloat16 [3, 3, 384, 384], replicated, may hold values from -0.109375 to 0.109375
- cotangent: bfloat16 [128, 32, 32, 384], P('tile', None, None, 'ch'), may hold values from -6 to 6
- edge_tiles: int32 [128, 4], replicated, may hold values from 0 to 127, as said below
- edge_turns: int32 [128, 4], replicated, may hold values from 0 to 3
- corner_tiles: int32 [128, 4], replicated, may hold values from 0 to 127, as said below
- corner_turns: int32 [128, 4], replicated, may hold values from 0 to 3
Outputs:
- output: bfloat16 [128, 32, 32, 384], P('tile', None, None, 'ch')
- grad_features: bfloat16 [128, 32, 32, 384], P('tile', None, None, 'ch')
- grad_weight: float32 [3, 3, 384, 384], P(None, None, 'ch')
Inputs may be any that keep to these rules, and one draw needn't show every extreme that they name: (edge_tiles[t, e] - t) mod 128 lies in 1 .. 4 or in 124 .. 127; both distances 4 and -4 occur. (corner_tiles[t, c] - t) mod 128 lies in 1 .. 4 or in 124 .. 127; both distances 4 and -4 occur.
All inputs are finite; a program needn't handle non-finite values.
Results may differ from a plain program's by a relative error of at most 0.0029.
Values may be sent and summed in bfloat16 or wider, within the bound.
A program may use at most 64 MiB of HBM per device.

v0:
```python
import math

import jax
import jax.numpy as jnp
import numpy as np
from jax import lax
from jax.sharding import PartitionSpec as P

SPAN = 4


def shifted(shard, axis, by):
    peers = lax.axis_size(axis)
    return lax.ppermute(shard, axis, [(i, (i + by) % peers) for i in range(peers)])


def turn_tables():
    labels = [[3 * row + col for col in range(3)] for row in range(3)]

    def turn_once(block):
        return [[block[col][2 - row] for col in range(3)] for row in range(3)]

    def sides_of(block):
        return [
            list(block[0]),
            [block[row][2] for row in range(3)],
            list(block[2]),
            [block[row][0] for row in range(3)],
        ]

    def corners_of(block):
        return [block[0][0], block[0][2], block[2][2], block[2][0]]

    base_sides = sides_of(labels)
    base_corners = corners_of(labels)
    edge_table = np.zeros((4, 4), np.int32)
    corner_table = np.zeros((4, 4), np.int32)
    for border in range(4):
        turned = labels
        for quarter in range(4):
            wanted = sides_of(turned)[(border + 2) % 4]
            for side_index in range(4):
                if base_sides[side_index] == wanted:
                    edge_table[border, quarter] = side_index
                if base_sides[side_index][::-1] == wanted:
                    edge_table[border, quarter] = side_index + 4
            corner_cell = corners_of(turned)[(border + 2) % 4]
            for corner_index in range(4):
                if base_corners[corner_index] == corner_cell:
                    corner_table[border, quarter] = corner_index
            turned = turn_once(turned)
    return (edge_table, corner_table)


def body(features, weight, cotangent, edge_tiles, edge_turns, corner_tiles, corner_turns):
    edge_table, corner_table = turn_tables()
    tile_count = lax.axis_size("tile")
    own_tile = lax.axis_index("tile")
    field = features[0]
    side_len = field.shape[0]
    chan_part = field.shape[2]
    chan_count = weight.shape[3]
    chan_start = lax.axis_index("ch") * chan_part
    rows = side_len * side_len
    offsets = list(range(-SPAN, 0)) + list(range(1, SPAN + 1))
    border_ids = jnp.arange(4)
    own_edges = edge_tiles[own_tile]
    own_corner_tiles = corner_tiles[own_tile]
    edge_slots = jnp.asarray(edge_table)[border_ids, edge_turns[own_tile]]
    corner_slots = jnp.asarray(corner_table)[border_ids, corner_turns[own_tile]]

    def position(target):
        wrapped = jnp.mod(target - own_tile, tile_count)
        signed = jnp.where(wrapped > tile_count // 2, wrapped - tile_count, wrapped)
        return jnp.where(signed < 0, signed + SPAN, signed + SPAN - 1)

    sides = jnp.stack([field[0], field[:, -1], field[-1], field[:, 0]])
    corners = jnp.stack([field[0, 0], field[0, -1], field[-1, -1], field[-1, 0]])
    got_sides = []
    got_corners = []
    for offset in offsets:
        near_sides, near_corners = shifted((sides, corners), "tile", -offset)
        got_sides.append(near_sides)
        got_corners.append(near_corners)
    all_sides = jnp.stack(got_sides)
    all_corners = jnp.stack(got_corners)
    edge_source = position(own_edges)
    corner_source = position(own_corner_tiles)
    halos = all_sides[edge_source, edge_slots % 4]
    halos = jnp.where((edge_slots >= 4)[:, None, None], halos[:, ::-1], halos)
    corner_halos = all_corners[corner_source, corner_slots]
    padded = jnp.pad(field, ((1, 1), (1, 1), (0, 0)))
    padded = padded.at[0, 1:-1].set(halos[0]).at[1:-1, -1].set(halos[1])
    padded = padded.at[-1, 1:-1].set(halos[2]).at[1:-1, 0].set(halos[3])
    padded = padded.at[0, 0].set(corner_halos[0]).at[0, -1].set(corner_halos[1])
    padded = padded.at[-1, -1].set(corner_halos[2]).at[-1, 0].set(corner_halos[3])
    taps = [(row_off, col_off) for row_off in range(3) for col_off in range(3)]
    blocks = [
        lax.dynamic_slice_in_dim(weight[row_off, col_off], chan_start, chan_part, 0)
        for row_off, col_off in taps
    ]
    windows = [
        padded[row_off : row_off + side_len, col_off : col_off + side_len].reshape(rows, chan_part)
        for row_off, col_off in taps
    ]
    partial_out = jnp.zeros((rows, chan_count), jnp.float32)
    for tap_index in range(9):
        partial_out = partial_out + jnp.dot(
            windows[tap_index], blocks[tap_index], preferred_element_type=jnp.float32
        )
    output = lax.psum_scatter(partial_out, "ch", scatter_dimension=1, tiled=True)
    output = output.astype(jnp.bfloat16).reshape(1, side_len, side_len, chan_part)
    cot_full = lax.all_gather(cotangent[0], "ch", axis=2, tiled=True).reshape(rows, chan_count)
    grad_padded = jnp.zeros(padded.shape, jnp.float32)
    grads = []
    for tap_index in range(9):
        row_off, col_off = taps[tap_index]
        back = lax.dot_general(
            cot_full,
            blocks[tap_index],
            (((1,), (1,)), ((), ())),
            preferred_element_type=jnp.float32,
        )
        grad_padded = grad_padded.at[
            row_off : row_off + side_len, col_off : col_off + side_len
        ].add(back.reshape(side_len, side_len, chan_part))
        grads.append(
            lax.dot_general(
                windows[tap_index],
                cot_full,
                (((0,), (0,)), ((), ())),
                preferred_element_type=jnp.float32,
            )
        )
    local_grad = jnp.stack(grads).reshape(3, 3, chan_part, chan_count)
    grad_weight = lax.psum(local_grad, "tile") * (1.0 / math.sqrt(tile_count * rows))
    pieces = jnp.stack(
        [grad_padded[0, 1:-1], grad_padded[1:-1, -1], grad_padded[-1, 1:-1], grad_padded[1:-1, 0]]
    ).astype(jnp.bfloat16)
    corner_pieces = jnp.stack(
        [grad_padded[0, 0], grad_padded[0, -1], grad_padded[-1, -1], grad_padded[-1, 0]]
    ).astype(jnp.bfloat16)
    slot_ids = jnp.arange(8)
    collected = jnp.zeros((8, side_len, chan_part), jnp.float32)
    corner_sums = jnp.zeros((4, chan_part), jnp.float32)
    for offset in offsets:
        got_pieces, got_corners = shifted((pieces, corner_pieces), "tile", offset)
        source = jnp.mod(own_tile - offset, tile_count)
        src_slots = jnp.asarray(edge_table)[border_ids, edge_turns[source]]
        src_corner_slots = jnp.asarray(corner_table)[border_ids, corner_turns[source]]
        edge_mine = edge_tiles[source] == own_tile
        corner_mine = corner_tiles[source] == own_tile
        hits = (edge_mine[:, None] & (src_slots[:, None] == slot_ids[None, :])).astype(jnp.bfloat16)
        corner_hits = (
            corner_mine[:, None] & (src_corner_slots[:, None] == border_ids[None, :])
        ).astype(jnp.bfloat16)
        collected = collected + jnp.einsum(
            "bk,bjc->kjc", hits, got_pieces, preferred_element_type=jnp.float32
        )
        corner_sums = corner_sums + jnp.einsum(
            "bk,bc->kc", corner_hits, got_corners, preferred_element_type=jnp.float32
        )
    side_sums = collected[:4] + collected[4:, ::-1]
    interior = grad_padded[1:-1, 1:-1]
    interior = interior.at[0].add(side_sums[0]).at[:, -1].add(side_sums[1])
    interior = interior.at[-1].add(side_sums[2]).at[:, 0].add(side_sums[3])
    interior = interior.at[0, 0].add(corner_sums[0]).at[0, -1].add(corner_sums[1])
    interior = interior.at[-1, -1].add(corner_sums[2]).at[-1, 0].add(corner_sums[3])
    grad_features = interior.astype(jnp.bfloat16)[None]
    return (output, grad_features, grad_weight)


def solution(mesh):
    return jax.shard_map(
        body,
        mesh=mesh,
        in_specs=(
            P("tile", None, None, "ch"),
            P(),
            P("tile", None, None, "ch"),
            P(),
            P(),
            P(),
            P(),
        ),
        out_specs=(
            P("tile", None, None, "ch"),
            P("tile", None, None, "ch"),
            P(None, None, "ch", None),
        ),
        check_vma=False,
    )
```

profile of v0, /device:TPU:1, one launch (start us, length us, event | category | flops | bytes accessed | tf_op | source)
XLA Modules:
  0.0 1410.9 jit_solution(13155073461944879584)
XLA Ops:
  22.5 38.2 %all-gather = bf16[1,32,32,384]{2,1,0,3:T(8,128)(2,1)} all-gather(bf16[1,32,32,192]{2,1,0,3:T(8,128)(2,1)S(1)} %copy.111), channel_id=2, replica_groups=mesh['tile'=128,'ch'=2] {'ch'}, dimensions={3}, use_global_device_ids=true | all-gather | bytes 1179648 | tf_op jit(solution)/shard_map/all_gather | solution.py:113
  60.7 4.5 copy.112
  74.4 6.4 scatter-add.59
  85.2 6.2 scatter-add.60
  100.6 4.9 scatter-add.61
  107.2 4.9 scatter-add.64
  121.3 4.9 scatter-add.65
  127.9 5.1 scatter-add.66
  137.6 4.9 scatter-add.69
  188.6 6.4 collective-permute-done.29
  198.6 6.6 collective-permute-start.27
  206.0 6.0 collective-permute-start.26
  217.9 6.7 collective-permute-done.8
  224.6 7.2 collective-permute-done.9
  231.8 6.6 collective-permute-done.10
  241.1 5.8 collective-permute-start.12
  247.7 6.0 collective-permute-start.13
  259.0 4.4 collective-permute-start.15
  264.1 6.2 collective-permute-start.24
  273.2 9.0 collective-permute-start.5
  286.6 3.8 collective-permute-start.23
  291.9 3.9 collective-permute-start.22
  323.9 5.8 collective-permute-start.18
  343.4 1054.2 %all-reduce.4.cloned.1.call-done = f32[3,3,192,384]{3,2,1,0:T(8,128)} async-done(((f32[3,3,192,384]{3,2,1,0:T(8,128)}), f32[3,3,192,384]{3,2,1,0:T(8,128)}) %all-reduce.4.cloned.1.call-update) | async-done | bytes 2654224 | tf_op jit(solution)/shard_map/psum | solution.py:136
  (351 shorter events, 175.2 us)
Async XLA Ops:
  8.0 1389.6 %all-reduce.4.cloned.1.call-start = ((), (), s32[]{:S(2)}) async-start(), calls=%async_computation.2 | async-start | bytes 5308416 | tf_op jit(solution)/shard_map/psum | solution.py:136
  10.5 262.7 %collective-permute-start = (bf16[4,32,192]{2,1,0:T(8,128)(2,1)}, bf16[4,32,192]{2,1,0:T(8,128)(2,1)}, u32[]{:S(2)}, u32[]{:S(2)}) collective-permute-start(bf16[4,32,192]{2,1,0:T(8,128)(2,1)} %pad_maximum_fusion), channel_id=1, source_target_pairs={{0,8},{2,10},{4,12},{6,14},{8,16},{10,18},{12,20},{14,22},{16,24},... | collective-permute-start | bytes 147464 | tf_op jit(solution)/shard_map/ppermute | solution.py:14
  14.2 269.4 %collective-permute-start.1 = (bf16[4,32,192]{2,1,0:T(8,128)(2,1)}, bf16[4,32,192]{2,1,0:T(8,128)(2,1)}, u32[]{:S(2)}, u32[]{:S(2)}) collective-permute-start(bf16[4,32,192]{2,1,0:T(8,128)(2,1)} %pad_maximum_fusion), channel_id=1, source_target_pairs={{0,6},{2,8},{4,10},{6,12},{8,14},{10,16},{12,18},{14,20},{16,22},{... | collective-permute-start | bytes 147464 | tf_op jit(solution)/shard_map/ppermute | solution.py:14
  16.0 269.1 %collective-permute-start.2 = (bf16[4,32,192]{2,1,0:T(8,128)(2,1)}, bf16[4,32,192]{2,1,0:T(8,128)(2,1)}, u32[]{:S(2)}, u32[]{:S(2)}) collective-permute-start(bf16[4,32,192]{2,1,0:T(8,128)(2,1)} %pad_maximum_fusion), channel_id=1, source_target_pairs={{0,4},{2,6},{4,8},{6,10},{8,12},{10,14},{12,16},{14,18},{16,20},{1... | collective-permute-start | bytes 147464 | tf_op jit(solution)/shard_map/ppermute | solution.py:14
  17.3 269.3 %collective-permute-start.3 = (bf16[4,32,192]{2,1,0:T(8,128)(2,1)}, bf16[4,32,192]{2,1,0:T(8,128)(2,1)}, u32[]{:S(2)}, u32[]{:S(2)}) collective-permute-start(bf16[4,32,192]{2,1,0:T(8,128)(2,1)} %pad_maximum_fusion), channel_id=1, source_target_pairs={{0,2},{2,4},{4,6},{6,8},{8,10},{10,12},{12,14},{14,16},{16,18},{18... | collective-permute-start | bytes 147464 | tf_op jit(solution)/shard_map/ppermute | solution.py:14
  149.0 32.0 %collective-permute-start.31 = (bf16[4,192]{1,0:T(4,128)(2,1)S(1)}, bf16[4,192]{1,0:T(4,128)(2,1)}, u32[]{:S(2)}, u32[]{:S(2)}) collective-permute-start(bf16[4,192]{1,0:T(4,128)(2,1)S(1)} %pad_maximum_fusion.3), channel_id=1, source_target_pairs={{0,8},{2,10},{4,12},{6,14},{8,16},{10,18},{12,20},{14,22},{16,24},... | collective-permute-start | bytes 4616 | tf_op jit(solution)/shard_map/ppermute | solution.py:14
  181.0 7.3 collective-permute-start.30
  198.6 7.4 collective-permute-start.27
  206.0 6.8 collective-permute-start.26
  217.2 7.3 collective-permute-start.8
  224.6 7.2 collective-permute-start.9
  247.7 6.8 collective-permute-start.13
  264.1 6.9 collective-permute-start.24
  271.1 20.8 %collective-permute-start.4 = (bf16[4,32,192]{2,1,0:T(8,128)(2,1)}, bf16[4,32,192]{2,1,0:T(8,128)(2,1)S(1)}, u32[]{:S(2)}, u32[]{:S(2)}) collective-permute-start(bf16[4,32,192]{2,1,0:T(8,128)(2,1)} %pad_maximum_fusion), channel_id=1, source_target_pairs={{0,254},{2,0},{4,2},{6,4},{8,6},{10,8},{12,10},{14,12},{16,14},{18... | collective-permute-start | bytes 147464 | tf_op jit(solution)/shard_map/ppermute | solution.py:14
  273.2 23.2 %collective-permute-start.5 = (bf16[4,32,192]{2,1,0:T(8,128)(2,1)}, bf16[4,32,192]{2,1,0:T(8,128)(2,1)S(1)}, u32[]{:S(2)}, u32[]{:S(2)}) collective-permute-start(bf16[4,32,192]{2,1,0:T(8,128)(2,1)} %pad_maximum_fusion), channel_id=1, source_target_pairs={{0,252},{2,254},{4,0},{6,2},{8,4},{10,6},{12,8},{14,10},{16,12},{1... | collective-permute-start | bytes 147464 | tf_op jit(solution)/shard_map/ppermute | solution.py:14
  283.6 13.4 collective-permute-start.6
  285.1 12.7 collective-permute-start.7
  286.6 37.3 %collective-permute-start.23 = (bf16[4,32,192]{2,0,1:T(4,128)(2,1)S(1)}, bf16[4,32,192]{2,0,1:T(4,128)(2,1)}, u32[]{:S(2)}, u32[]{:S(2)}) collective-permute-start(bf16[4,32,192]{2,0,1:T(4,128)(2,1)S(1)} %pad_maximum_fusion.1), channel_id=1, source_target_pairs={{0,8},{2,10},{4,12},{6,14},{8,16},{10,18},{12,20},{14,22},{16,24},... | collective-permute-start | bytes 147464 | tf_op jit(solution)/shard_map/ppermute | solution.py:14
  291.9 39.0 %collective-permute-start.22 = (bf16[4,32,192]{2,0,1:T(4,128)(2,1)S(1)}, bf16[4,32,192]{2,0,1:T(4,128)(2,1)}, u32[]{:S(2)}, u32[]{:S(2)}) collective-permute-start(bf16[4,32,192]{2,0,1:T(4,128)(2,1)S(1)} %pad_maximum_fusion.1), channel_id=1, source_target_pairs={{0,6},{2,8},{4,10},{6,12},{8,14},{10,16},{12,18},{14,20},{16,22},{... | collective-permute-start | bytes 147464 | tf_op jit(solution)/shard_map/ppermute | solution.py:14
  296.4 36.0 %collective-permute-start.21 = (bf16[4,32,192]{2,0,1:T(4,128)(2,1)S(1)}, bf16[4,32,192]{2,0,1:T(4,128)(2,1)S(1)}, u32[]{:S(2)}, u32[]{:S(2)}) collective-permute-start(bf16[4,32,192]{2,0,1:T(4,128)(2,1)S(1)} %pad_maximum_fusion.1), channel_id=1, source_target_pairs={{0,4},{2,6},{4,8},{6,10},{8,12},{10,14},{12,16},{14,18},{16,20},{1... | collective-permute-start | bytes 147464 | tf_op jit(solution)/shard_map/ppermute | solution.py:14
  297.0 35.8 %collective-permute-start.20 = (bf16[4,32,192]{2,0,1:T(4,128)(2,1)S(1)}, bf16[4,32,192]{2,0,1:T(4,128)(2,1)}, u32[]{:S(2)}, u32[]{:S(2)}) collective-permute-start(bf16[4,32,192]{2,0,1:T(4,128)(2,1)S(1)} %pad_maximum_fusion.1), channel_id=1, source_target_pairs={{0,2},{2,4},{4,6},{6,8},{8,10},{10,12},{12,14},{14,16},{16,18},{18... | collective-permute-start | bytes 147464 | tf_op jit(solution)/shard_map/ppermute | solution.py:14
  297.8 36.1 %collective-permute-start.19 = (bf16[4,32,192]{2,0,1:T(4,128)(2,1)S(1)}, bf16[4,32,192]{2,0,1:T(4,128)(2,1)}, u32[]{:S(2)}, u32[]{:S(2)}) collective-permute-start(bf16[4,32,192]{2,0,1:T(4,128)(2,1)S(1)} %pad_maximum_fusion.1), channel_id=1, source_target_pairs={{0,254},{2,0},{4,2},{6,4},{8,6},{10,8},{12,10},{14,12},{16,14},{18... | collective-permute-start | bytes 147464 | tf_op jit(solution)/shard_map/ppermute | solution.py:14
  313.9 1087.2 %reduce-scatter.2.cloned.1.call-start = ((), (), s32[]{:S(2)}) async-start(), calls=%async_computation.1 | async-start | bytes 2359296 | tf_op jit(solution)/shard_map/reduce_scatter | solution.py:111
  323.9 11.2 collective-permute-start.18
  (62 other events, 509.6 us)
Sparse Core Ops, SparseCore 0:
  314.0 1083.5 all-reduce.3
Sparse Core Ops, SparseCore 1:
  324.0 38.1 reduce-scatter.1
where the time goes:
time: 1420 us; the launch traced here: 1410 us
  waiting for transfers between devices  1100 us (77%)
  local copies, waits for them, and re-layouts  114 us (8%)
  starting transfers between devices  77.9 us (5%)
  blocking collectives  38.2 us (3%)
  other arithmetic  34.5 us (2%)
  matrix products  28.4 us (2%)
  between operations  17.1 us (1%)
    psum x1, waiting for transfers between devices, body(): lax.psum(local_grad, 'tile') * (1.0 / math.sqrt(tile_count * rows))  1050 us
    ppermute x32, starting transfers between devices, shifted(): lax.ppermute(shard, axis, [(i, (i + by) % peers) for i in range(peers)])  77.8 us
    ppermute x32, waiting for transfers between devices, shifted(): lax.ppermute(shard, axis, [(i, (i + by) % peers) for i in range(peers)])  46.7 us
    scatter-add x9, local copies, waits for them, and re-layouts, body(): grad_padded = grad_padded.at[row_off:row_off + side_len, col_off:col_off...  39.5 us
    all_gather x1, blocking collectives, body(): lax.all_gather(cotangent[0], 'ch', axis=2, tiled=True)  38.2 us
  transfers between devices with their start and end apart: 34, of which 18 were waited for; matrix products, arithmetic and copies ran while one was open for 12% of the time, Pallas kernels for 0%

commit v1 on v0

v1 whole, which is shorter than its diff:
```python
import math

import jax
import jax.numpy as jnp
import numpy as np
from jax import lax
from jax.experimental import pallas as pl
from jax.experimental.pallas import tpu as pltpu
from jax.sharding import PartitionSpec as P

MESH = pl.DeviceIdType.MESH
SPAN = 4
OFFSETS = [-4, -3, -2, -1, 1, 2, 3, 4]
S = 32
ROWS = S * S
UNIT = 16
VM = pltpu.VMEM
BF = jnp.bfloat16
F32 = jnp.float32


def turn_tables():
    labels = [[3 * row + col for col in range(3)] for row in range(3)]

    def turn_once(block):
        return [[block[col][2 - row] for col in range(3)] for row in range(3)]

    def sides_of(block):
        return [
            list(block[0]),
            [block[row][2] for row in range(3)],
            list(block[2]),
            [block[row][0] for row in range(3)],
        ]

    def corners_of(block):
        return [block[0][0], block[0][2], block[2][2], block[2][0]]

    base_sides = sides_of(labels)
    base_corners = corners_of(labels)
    edge_table = np.zeros((4, 4), np.int32)
    corner_table = np.zeros((4, 4), np.int32)
    for border in range(4):
        turned = labels
        for quarter in range(4):
            wanted = sides_of(turned)[(border + 2) % 4]
            for side_index in range(4):
                if base_sides[side_index] == wanted:
                    edge_table[border, quarter] = side_index
                if base_sides[side_index][::-1] == wanted:
                    edge_table[border, quarter] = side_index + 4
            corner_cell = corners_of(turned)[(border + 2) % 4]
            for corner_index in range(4):
                if base_corners[corner_index] == corner_cell:
                    corner_table[border, quarter] = corner_index
            turned = turn_once(turned)
    return (edge_table, corner_table)


EDGE_TABLE, CORNER_TABLE = turn_tables()


def lookup(table, border, turn):
    row = [int(v) for v in table[border]]
    value = jnp.int32(row[0])
    for quarter in range(1, 4):
        value = jnp.where(turn == quarter, jnp.int32(row[quarter]), value)
    return value


def slot_of(offset):
    return offset + SPAN if offset < 0 else offset + SPAN - 1


def wrap(index, size):
    return lax.rem(index + size, jnp.int32(size))


def coords():
    tile = lax.axis_index("tile")
    ch = lax.axis_index("ch")
    core = lax.rem(tile, 2)
    y = lax.rem(tile // 2, 4)
    xl = lax.rem(tile // 8, 2)
    z = tile // 16
    return tile, ch, core, y, xl, z


def dev(tile, ch):
    return {"tile": tile, "ch": ch}


def x_neighbours(tile, ch, xl):
    beside = tile + 8 - 16 * xl
    return dev(beside, ch), dev(beside, 1 - ch)


def remote(src, dst, send, recv, where):
    return pltpu.make_async_remote_copy(
        src_ref=src, dst_ref=dst, send_sem=send, recv_sem=recv, device_id=where, device_id_type=MESH
    )


class Swap:
    def __init__(self, src, dst, relay, sems, tile, ch, xl):
        self.n = relay.shape[1]
        near, far = x_neighbours(tile, ch, xl)
        self.first, self.second = [], []
        for i in range(self.n):
            for path in range(2):
                hop1, hop2 = (near, far) if path == 0 else (far, near)
                j = path * self.n + i
                self.first.append(remote(src.at[j], relay.at[path, i], sems.at[0, j], sems.at[1, j], hop1))
                self.second.append(remote(relay.at[path, i], dst.at[j], sems.at[2, j], sems.at[3, j], hop2))

    def start(self):
        for copy in self.first:
            copy.start()

    def relay(self):
        for one, two in zip(self.first, self.second):
            one.wait_recv()
            two.start()

    def finish(self):
        for one, two in zip(self.first, self.second):
            one.wait_send()
            two.wait()


def barrier(devices):
    sem = pltpu.get_barrier_semaphore()
    for where in devices:
        pl.semaphore_signal(sem, inc=1, device_id=where, device_id_type=MESH)
    pl.semaphore_wait(sem, len(devices))


def near_copies(src, dst, sems, tile, ch, tiles):
    copies = []
    for offset in OFFSETS:
        k = slot_of(-offset)
        copies.append(
            remote(src, dst.at[k], sems.at[0, k], sems.at[1, k], dev(wrap(tile + offset, tiles), ch))
        )
    return copies


def exchange_kernel(sides, cot, all_sides, cot_other, relay, near_sems, swap_sems):
    tiles = 128
    tile, ch, core, y, xl, z = coords()
    near, far = x_neighbours(tile, ch, xl)
    barrier([dev(wrap(tile + o, tiles), ch) for o in OFFSETS] + [near, far])
    swap = Swap(cot, cot_other, relay, swap_sems, tile, ch, xl)
    copies = near_copies(sides, all_sides, near_sems, tile, ch, tiles)
    swap.start()
    for copy in copies:
        copy.start()
    swap.relay()
    for copy in copies:
        copy.wait()
    swap.finish()


def iota2(shape, dim):
    return lax.broadcasted_iota(jnp.int32, shape, dim)


def flipper(rev):
    ii = iota2((S, S), 0)
    target = jnp.where(rev == 1, S - 1 - ii, ii)
    return jnp.where(iota2((S, S), 1) == target, 1.0, 0.0).astype(BF)


def source_slot(target, tile, tiles):
    away = wrap(target - tile, tiles)
    return jnp.where(away > tiles // 2, away - tiles + SPAN, away + SPAN - 1)


def spread_columns(buf, row, x, left, right):
    io = iota2(x.shape, 0)
    buf[0, row] = jnp.where(io == 0, left, pltpu.roll(x, 1, 0)).astype(BF)
    buf[2, row] = jnp.where(io == S - 1, right, pltpu.roll(x, S - 1, 0)).astype(BF)


def compute_kernel(
    edge_tiles, edge_turns, corner_tiles, corner_turns,
    feat, all_sides, cot, cot_other, weight,
    grads, padded, columns, interior, pieces,
    halo, cots, cot_columns,
):
    tiles = 128
    tile, ch, core, y, xl, z = coords()
    C2 = feat.shape[2]
    for border in range(4):
        source = source_slot(edge_tiles[tile, border], tile, tiles)
        slot = lookup(EDGE_TABLE, border, edge_turns[tile, border])
        rev = slot // 4
        halo[border] = jnp.dot(
            flipper(rev), all_sides[source, slot - 4 * rev], preferred_element_type=F32
        )
    columns[0, 1 : S + 1] = halo[3]
    columns[1, 1 : S + 1] = halo[1]
    for corner in range(4):
        source = source_slot(corner_tiles[tile, corner], tile, tiles)
        slot = lookup(CORNER_TABLE, corner, corner_turns[tile, corner])
        side = jnp.where(slot < 2, 0, 2)
        row = jnp.where((slot == 0) | (slot == 3), 0, S - 1)
        cells = all_sides[source, side].astype(F32)
        value = jnp.sum(jnp.where(iota2(cells.shape, 0) == row, cells, 0.0), axis=0, keepdims=True)
        at = 0 if corner < 2 else S + 1
        columns[(0, 1, 1, 0)[corner], at : at + 1] = value
    padded[1, 0] = halo[0].astype(BF)
    padded[1, S + 1] = halo[2].astype(BF)
    padded[1, 1 : S + 1] = feat[...]

    def shift_features(row, carry):
        x = padded[1, row].astype(F32)
        spread_columns(padded, row, x, columns[0, pl.ds(row, 1)], columns[1, pl.ds(row, 1)])
        return carry

    lax.fori_loop(0, S + 2, shift_features, 0)

    zero = jnp.zeros((S, 2 * C2), BF)
    for part in range(3):
        for row in (0, 1, S + 2, S + 3):
            cots[part, row] = zero
    cot_columns[...] = jnp.zeros_like(cot_columns)

    def shift_cots(row, carry):
        own = cot[row].astype(F32)
        other = cot_other[row].astype(F32)
        x = jnp.where(ch == 0, jnp.concatenate([own, other], axis=1), jnp.concatenate([other, own], axis=1))
        cots[1, row + 2] = x.astype(BF)
        nothing = jnp.zeros((1, 2 * C2), F32)
        spread_columns(cots, row + 2, x, nothing, nothing)
        cot_columns[0, pl.ds(row + 2, 1)] = x[0:1]
        cot_columns[1, pl.ds(row + 2, 1)] = x[S - 1 : S]
        return carry

    lax.fori_loop(0, S, shift_cots, 0)

    def weight_grad(tap, carry):
        a, b = tap // 3, lax.rem(tap, 3)
        window = padded[b, pl.ds(a, S)].reshape(ROWS, C2)
        full = cots[1, 2 : S + 2].reshape(ROWS, 2 * C2)
        part = lax.dot_general(window, full, (((0,), (0,)), ((), ())), preferred_element_type=F32)
        at = pl.multiple_of(tap * (C2 // 2), 32)
        grads[0, pl.ds(at, C2 // 2)] = part[: C2 // 2]
        grads[1, pl.ds(at, C2 // 2)] = part[C2 // 2 :]
        return carry

    lax.fori_loop(0, 9, weight_grad, 0)
    tail = grads.shape[1] - 9 * (C2 // 2)
    grads[:, 9 * (C2 // 2) :] = jnp.zeros((2, tail, 2 * C2), F32)

    nt = (((1,), (1,)), ((), ()))
    half = (S + 2) // 2

    def feature_grad(block, carry):
        total = None
        for a in range(3):
            for b in range(3):
                window = cots[2 - b, pl.ds(block * half + 2 - a, half)].reshape(half * S, 2 * C2)
                term = lax.dot_general(window, weight[3 * a + b], nt, preferred_element_type=F32)
                total = term if total is None else total + term
        interior[pl.ds(block * half, half)] = total.reshape(half, S, C2)
        return carry

    lax.fori_loop(0, 2, feature_grad, 0)
    pieces[0] = interior[0].astype(BF)
    pieces[2] = interior[S + 1].astype(BF)
    ends = []
    for side in range(2):
        total = None
        for a in range(3):
            line = cot_columns[side, 2 - a : 2 - a + 40].astype(BF)
            term = lax.dot_general(line, weight[3 * a + 2 * side], nt, preferred_element_type=F32)
            total = term if total is None else total + term
        cot_columns[side, 0:40, 0:C2] = total
        pieces[3 - 2 * side] = cot_columns[side, 1 : S + 1, 0:C2].astype(BF)
        ends.append((total[0:1], total[S + 1 : S + 2]))
    io = iota2((S, C2), 0)
    corner_rows = jnp.zeros((S, C2), F32)
    for corner, value in enumerate((ends[0][0], ends[1][0], ends[1][1], ends[0][1])):
        corner_rows = jnp.where(io == corner, value, corner_rows)
    pieces[4] = corner_rows.astype(BF)


def reduce_kernel(
    scale, grads, padded, pieces,
    gathered, padded_other, all_pieces,
    pair_in, y_out, y_in, acc, x_in, z_out, z_in, relay,
    near_sems, swap_sems, pair_sems, y_sems, x_sems, z_sems, gz_sems, gx_sems, gy_sems, gp_sems,
):
    tiles = 128
    tile, ch, core, y, xl, z = coords()
    near, far = x_neighbours(tile, ch, xl)
    pair = dev(tile + 1 - 2 * core, ch)
    y_at = [lax.rem(y + 1 + j, 4) for j in range(3)]
    y_peer = [dev(tile + 2 * (q - y), ch) for q in y_at]
    z_at = [lax.rem(z + 1 + j, 8) for j in range(7)]
    z_peer = [dev(tile + 16 * (q - z), ch) for q in z_at]
    barrier(
        [dev(wrap(tile + o, tiles), ch) for o in OFFSETS] + [near, far, pair] + y_peer + z_peer
    )
    order = y_at + [y]
    pair_copies = [
        remote(grads.at[1 - core, q], pair_in.at[j], pair_sems.at[0, j], pair_sems.at[1, j], pair)
        for j, q in enumerate(order)
    ]
    for copy in pair_copies:
        copy.start()
    swap = Swap(padded, padded_other, relay, swap_sems, tile, ch, xl)
    swap.start()
    copies = near_copies(pieces, all_pieces, near_sems, tile, ch, tiles)
    y_copies = [
        remote(y_out.at[j], y_in.at[j], y_sems.at[0, j], y_sems.at[1, j], y_peer[j]) for j in range(3)
    ]
    for j in range(4):
        pair_copies[j].wait_recv()
        total = grads[core, order[j]] + pair_in[j]
        if j < 3:
            y_out[j] = total.astype(BF)
            y_copies[j].start()
        else:
            acc[...] = total.reshape(acc.shape)
    swap.relay()
    for copy in copies:
        copy.start()
    for j in range(3):
        y_copies[j].wait_recv()
        acc[...] += y_in[j].astype(F32).reshape(acc.shape)
    x_copy = remote(acc.at[1 - xl], x_in, x_sems.at[0], x_sems.at[1], near)
    x_copy.start()
    z_out[7] = jnp.zeros(z_out.shape[1:], F32)
    x_copy.wait_recv()
    z_out[0:7] = (acc[xl] + x_in[...]).reshape(7, UNIT, acc.shape[2])
    z_copies = [
        remote(z_out.at[z_at[j]], z_in.at[j], z_sems.at[0, j], z_sems.at[1, j], z_peer[j])
        for j in range(7)
    ]
    for copy in z_copies:
        copy.start()
    total = z_out[z]
    for j in range(7):
        z_copies[j].wait_recv()
        total = total + z_in[j]
    gathered[core, y, xl, z] = (total * scale).astype(BF)
    spot = gathered.at[core, y, xl, z]
    gz_copies = [
        remote(spot, spot, gz_sems.at[0, j], gz_sems.at[1, j], z_peer[j]) for j in range(7)
    ]
    for copy in gz_copies:
        copy.start()
    for copy in gz_copies:
        copy.wait_recv()
    spot = gathered.at[core, y, xl]
    gx_copy = remote(spot, spot, gx_sems.at[0], gx_sems.at[1], near)
    gx_copy.start()
    gx_copy.wait_recv()
    spot = gathered.at[core, y]
    gy_copies = [remote(spot, spot, gy_sems.at[0, j], gy_sems.at[1, j], y_peer[j]) for j in range(3)]
    for copy in gy_copies:
        copy.start()
    gp_copies = []
    for j in range(4):
        q = y if j == 0 else lax.rem(y + 4 - j, 4)
        if j > 0:
            gy_copies[j - 1].wait_recv()
        spot = gathered.at[core, q]
        gp_copies.append(remote(spot, spot, gp_sems.at[0, j], gp_sems.at[1, j], pair))
        gp_copies[j].start()
    for copy in copies:
        copy.wait()
    swap.finish()
    for copy in gp_copies:
        copy.wait()
    x_copy.wait_send()
    gx_copy.wait_send()
    for copy in pair_copies + y_copies + z_copies + gz_copies + gy_copies:
        copy.wait_send()


def final_kernel(
    edge_tiles, edge_turns, corner_tiles, corner_turns,
    interior, all_pieces, padded, padded_other, weight,
    output, grad_features,
    sums, corner_sums, shifted,
):
    tiles = 128
    tile, ch, core, y, xl, z = coords()
    C2 = interior.shape[2]
    sums[...] = jnp.zeros_like(sums)
    corner_sums[...] = jnp.zeros_like(corner_sums)
    for offset in OFFSETS:
        k = slot_of(-offset)
        source = wrap(tile - offset, tiles)
        for border in range(4):

            @pl.when(edge_tiles[source, border] == tile)
            def _():
                slot = lookup(EDGE_TABLE, border, edge_turns[source, border])
                rev = slot // 4
                sums[slot - 4 * rev] += jnp.dot(
                    flipper(rev), all_pieces[k, border], preferred_element_type=F32
                )

            @pl.when(corner_tiles[source, border] == tile)
            def _():
                slot = lookup(CORNER_TABLE, border, corner_turns[source, border])
                cells = all_pieces[k, 4].astype(F32)
                value = jnp.sum(
                    jnp.where(iota2(cells.shape, 0) == border, cells, 0.0), axis=0, keepdims=True
                )
                corner_sums[slot] += jnp.broadcast_to(value, (8, C2))

    io = iota2((S, C2), 0)
    for corner in range(4):
        at = 0 if corner in (0, 3) else S - 1
        side = 0 if corner < 2 else 2
        sums[side] += jnp.where(io == at, corner_sums[corner, 0:1], 0.0)

    def add_sides(row, carry):
        x = interior[row + 1]
        x = x + jnp.where(io == 0, sums[3, pl.ds(row, 1)], 0.0)
        x = x + jnp.where(io == S - 1, sums[1, pl.ds(row, 1)], 0.0)
        x = x + jnp.where(row == 0, sums[0], 0.0)
        x = x + jnp.where(row == S - 1, sums[2], 0.0)
        grad_features[row] = x.astype(BF)
        return carry

    lax.fori_loop(0, S, add_sides, 0)

    sums[...] = jnp.zeros_like(sums)
    edge = padded_other[S + 2].astype(F32)
    edge2 = padded_other[S + 3].astype(F32)
    corners = padded_other[S + 4].astype(F32)
    shifted[1] = padded_other[0 : S + 2]

    def shift_features(row, carry):
        x = shifted[1, row].astype(F32)
        hot = iota2((S, C2), 0) == row - 1
        left = jnp.sum(jnp.where(hot, edge, 0.0), axis=0, keepdims=True)
        right = jnp.sum(jnp.where(hot, edge2, 0.0), axis=0, keepdims=True)
        left = left + jnp.where(row == 0, corners[0:1], 0.0) + jnp.where(row == S + 1, corners[3:4], 0.0)
        right = right + jnp.where(row == 0, corners[1:2], 0.0) + jnp.where(row == S + 1, corners[2:3], 0.0)
        spread_columns(shifted, row, x, left, right)
        return carry

    lax.fori_loop(0, S + 2, shift_features, 0)
    half = S // 2

    def convolve(block, carry):
        total = None
        for a in range(3):
            for b in range(3):
                for buf, part in ((padded, 0), (shifted, 1)):
                    window = buf[b, pl.ds(block * half + a, half)].reshape(half * S, C2)
                    term = jnp.dot(window, weight[part, 3 * a + b], preferred_element_type=F32)
                    total = term if total is None else total + term
        output[pl.ds(block * half, half)] = total.reshape(half, S, C2).astype(BF)
        return carry

    lax.fori_loop(0, 2, convolve, 0)


def params(**more):
    return pltpu.CompilerParams(vmem_limit_bytes=60 * 1024 * 1024, **more)


VSPEC = pl.BlockSpec(memory_space=VM)
SSPEC = pl.BlockSpec(memory_space=pltpu.SMEM)
DMA = pltpu.SemaphoreType.DMA


def body(features, weight, cotangent, edge_tiles, edge_turns, corner_tiles, corner_turns):
    field = features[0]
    C2 = field.shape[2]
    C = 2 * C2
    ch = lax.axis_index("ch")
    cot = cotangent[0]
    shape = jax.ShapeDtypeStruct
    sides = jnp.stack([field[0], field[:, -1], field[-1], field[:, 0]])

    all_sides, cot_other = pl.pallas_call(
        exchange_kernel,
        name="exchange",
        out_shape=(shape((8, 4, S, C2), BF), shape((8, ROWS // 8, C2), BF)),
        in_specs=[VSPEC] * 2,
        out_specs=(VSPEC,) * 2,
        scratch_shapes=[VM((2, 4, ROWS // 8, C2), BF), DMA((2, 8)), DMA((4, 8))],
        compiler_params=params(collective_id=0, has_side_effects=True),
    )(sides, cot.reshape(8, ROWS // 8, C2))

    taps = weight.reshape(9, C, C)
    weight_rows = lax.dynamic_slice_in_dim(taps, ch * C2, C2, 1)
    out_columns = lax.dynamic_slice_in_dim(taps, ch * C2, C2, 2)
    out_columns = jnp.stack(
        [
            lax.dynamic_slice_in_dim(out_columns, ch * C2, C2, 1),
            lax.dynamic_slice_in_dim(out_columns, (1 - ch) * C2, C2, 1),
        ]
    )
    tables = (edge_tiles, edge_turns, corner_tiles, corner_turns)
    grads, padded, columns, interior, pieces = pl.pallas_call(
        compute_kernel,
        name="compute",
        out_shape=(
            shape((2, 56 * UNIT, C), F32),
            shape((3, S + 2, S, C2), BF),
            shape((2, 40, C2), F32),
            shape((S + 2, S, C2), F32),
            shape((5, S, C2), BF),
        ),
        in_specs=[SSPEC] * 4 + [VSPEC] * 5,
        out_specs=(VSPEC,) * 5,
        scratch_shapes=[VM((4, S, C2), F32), VM((3, S + 4, S, C), BF), VM((2, 48, C), F32)],
        compiler_params=params(),
    )(*tables, field, all_sides, cot, cot_other.reshape(S, S, C2), weight_rows)

    lines = columns[:, 1 : S + 1].astype(BF)
    ends = jnp.concatenate([columns[:, 0], columns[::-1, S + 1]]).astype(BF)
    ends = jnp.pad(ends, ((0, S - 4), (0, 0)))[None]
    sent = jnp.concatenate([padded[1], lines, ends, jnp.zeros((3, S, C2), BF)]).reshape(8, 5, S, C2)

    gathered, padded_other, all_pieces = pl.pallas_call(
        lambda *refs: reduce_kernel(1.0 / math.sqrt(128 * ROWS), *refs),
        name="reduce",
        out_shape=(
            shape((2, 4, 2, 8, UNIT, C), BF),
            shape((8, 5, S, C2), BF),
            shape((8, 5, S, C2), BF),
        ),
        in_specs=[VSPEC] * 3,
        out_specs=(VSPEC,) * 3,
        scratch_shapes=[
            VM((4, 14 * UNIT, C), F32),
            VM((3, 14 * UNIT, C), BF),
            VM((3, 14 * UNIT, C), BF),
            VM((2, 7 * UNIT, C), F32),
            VM((7 * UNIT, C), F32),
            VM((8, UNIT, C), F32),
            VM((7, UNIT, C), F32),
            VM((2, 4, 5, S, C2), BF),
            DMA((2, 8)),
            DMA((4, 8)),
            DMA((2, 4)),
            DMA((2, 3)),
            DMA((2,)),
            DMA((2, 7)),
            DMA((2, 7)),
            DMA((2,)),
            DMA((2, 3)),
            DMA((2, 4)),
        ],
        compiler_params=params(collective_id=1, has_side_effects=True),
    )(grads.reshape(2, 4, 14 * UNIT, C), sent, pieces)

    output, grad_features = pl.pallas_call(
        final_kernel,
        name="final",
        out_shape=(shape((S, S, C2), BF), shape((S, S, C2), BF)),
        in_specs=[SSPEC] * 4 + [VSPEC] * 5,
        out_specs=(VSPEC,) * 2,
        scratch_shapes=[VM((4, S, C2), F32), VM((4, 8, C2), F32), VM((3, S + 2, S, C2), BF)],
        compiler_params=params(),
    )(*tables, interior, all_pieces, padded, padded_other.reshape(8 * 5, S, C2), out_columns)

    flat = gathered[:, :, :, :7].reshape(2, 56 * UNIT, C)[:, : 9 * (C2 // 2)]
    grad_weight = flat.reshape(2, 9, C2 // 2, C).transpose(1, 0, 2, 3).astype(F32).reshape(3, 3, C2, C)
    return (output[None], grad_features[None], grad_weight)


def solution(mesh):
    return jax.shard_map(
        body,
        mesh=mesh,
        in_specs=(
            P("tile", None, None, "ch"),
            P(),
            P("tile", None, None, "ch"),
            P(),
            P(),
            P(),
            P(),
        ),
        out_specs=(
            P("tile", None, None, "ch"),
            P("tile", None, None, "ch"),
            P(None, None, "ch", None),
        ),
        check_vma=False,
    )
```

time: 1420 us -> 137 us (0.10)
  waiting for transfers between devices: 1100 us -> 0 us
  Pallas kernels: 0 us -> 116 us
  local copies, waits for them, and re-layouts: 114 us -> 15.5 us
  starting transfers between devices: 77.9 us -> 0 us
  blocking collectives: 38.2 us -> 0 us
  other arithmetic: 34.5 us -> 4.09 us
  matrix products: 28.4 us -> 0 us
  between operations: 17.1 us -> 0.75 us
    psum x1 -> x0, waiting for transfers between devices: 1050 us -> none  [body(): lax.psum(local_grad, 'tile') * (1.0 / math.sqrt(tile_count * rows))]
    pallas_call x0 -> x4, Pallas kernels: none -> 116 us  [the longest x1 62.9 us: body(): pl.pallas_call(lambda *refs: reduce_kernel(1.0 / math.sqrt(128 * ROWS), *...]
    ppermute x32 -> x0, starting transfers between devices: 77.8 us -> none  [shifted(): lax.ppermute(shard, axis, [(i, (i + by) % peers) for i in range(peers)])]
    ppermute x32 -> x0, waiting for transfers between devices: 46.7 us -> none  [shifted(): lax.ppermute(shard, axis, [(i, (i + by) % peers) for i in range(peers)])]
    scatter-add x16 -> x0, local copies, waits for them, and re-layouts: 41.2 us -> none  [the longest x9 39.5 us: body(): grad_padded = grad_padded.at[row_off:row_off + side_len, col_off:col_off...]
    all_gather x1 -> x0, blocking collectives: 38.2 us -> none  [body(): lax.all_gather(cotangent[0], 'ch', axis=2, tiled=True)]
    dot_general x43 -> x0, matrix products: 28.4 us -> none  [the longest x9 10.1 us: body(): lax.dot_general(cot_full, blocks[tap_index], (((1,), (1,)), ((), ())), pr...]
    gather x20 -> x0, local copies, waits for them, and re-layouts: 18.1 us -> none  [the longest x8 9.5 us: body(): src_slots = jnp.asarray(edge_table)[border_ids, edge_turns[source]]]
  transfers between devices with their start and end apart: 34 -> 0, of which waited for: 18 -> 0; matrix products, arithmetic and copies ran while one was open for 12% -> 0% of each run, Pallas kernels for 0% -> 0%
where the time goes in v1:
time: 137 us; the launch traced here: 136 us
  Pallas kernels  116 us (85%)
  local copies, waits for them, and re-layouts  15.5 us (11%)
  other arithmetic  4.09 us (3%)
    pallas_call x1, Pallas kernels, body(): pl.pallas_call(lambda *refs: reduce_kernel(1.0 / math.sqrt(128 * ROWS), *...  62.9 us
    pallas_call x1, Pallas kernels, body(): pl.pallas_call(exchange_kernel, name='exchange', out_shape=(shape((8, 4,...  25.4 us
    pallas_call x1, Pallas kernels, body(): pl.pallas_call(compute_kernel, name='compute', out_shape=(shape((2, 56 *...  16.4 us
    pallas_call x1, Pallas kernels, body(): pl.pallas_call(final_kernel, name='final', out_shape=(shape((S, S, C2), B...  10.9 us
    unnamed x11, local copies, waits for them, and re-layouts  5.63 us

profile of v1, /device:TPU:1, one launch (start us, length us, event | category | flops | bytes accessed | tf_op | source)
XLA Modules:
  0.0 136.0 jit_solution(9421314847097788838)
XLA Ops:
  0.6 1.4 %copy.35.edge_tiles = s32[128,4]{1,0:T(8,128)} copy(s32[128,4]{0,1:T(4,128)} %param.10) | data formatting | bytes 4096 | tf_op args[3]
  2.0 1.4 %copy.36.edge_turns = s32[128,4]{1,0:T(8,128)} copy(s32[128,4]{0,1:T(4,128)} %param.11) | data formatting | bytes 4096 | tf_op args[4]
  3.4 1.4 %copy.37.corner_tiles = s32[128,4]{1,0:T(8,128)} copy(s32[128,4]{0,1:T(4,128)} %param.12) | data formatting | bytes 4096 | tf_op args[5]
  4.8 1.4 %copy.38.corner_turns = s32[128,4]{1,0:T(8,128)} copy(s32[128,4]{0,1:T(4,128)} %param.13) | data formatting | bytes 4096 | tf_op args[6]
  6.2 1.0 fusion.4
  7.3 0.7 slice_bitcast_fusion.2
  8.0 0.6 pad_maximum_fusion.1.sides
  8.7 25.4 %exchange.1 = (bf16[8,4,32,192]{3,2,1,0:T(8,128)(2,1)}, bf16[8,128,192]{2,1,0:T(8,128)(2,1)}) custom-call(bf16[4,32,192]{2,1,0:T(8,128)(2,1)} %pad_maximum_fusion.1.sides, bf16[8,128,192]{2,1,0:T(8,128)(2,1)} %bitcast.45), custom_call_target="tpu_custom_call" | custom-call | tf_op jit(solution)/shard_map/exchange/pallas_call | solution.py:485
  34.1 2.5 %constant_dynamic-slice_fusion.weight = bf16[9,192,384]{2,1,0:T(8,128)(2,1)} fusion(bf16[9,384,384]{2,1,0:T(8,128)(2,1)} %bitcast.40, s32[]{:T(128)S(6)} %select_n.12), kind=kLoop, calls=%fused_computation.18 | loop fusion | bytes 2654212 | tf_op jit(solution)/shard_map/dynamic_slice | solution.py:496
  36.6 16.4 %compute.1 = (f32[2,896,384]{2,1,0:T(8,128)}, bf16[3,34,32,192]{3,2,1,0:T(8,128)(2,1)}, f32[2,40,192]{2,1,0:T(8,128)}, f32[34,32,192]{2,1,0:T(8,128)}, bf16[5,32,192]{2,1,0:T(8,128)(2,1)}) custom-call(s32[128,4]{1,0:T(8,128)} %copy.35.edge_tiles, s32[128,4]{1,0:T(8,128)} %copy.36.edge_turns, s32[128,4]{1,0:T(8,128)} %copy.37.corner_tiles, ...), custom_call_target="tpu_custom_call" | custom-call | tf_op jit(solution)/shard_map/compute/pallas_call | solution.py:505
  53.0 0.7 slice.47
  53.8 0.9 convert.13
  54.7 1.1 slice_bitcast_fusion
  55.8 0.1 pad.10.clone
  55.9 1.0 maximum_maximum_fusion
  56.9 62.9 %reduce.1 = (bf16[2,4,2,8,16,384]{5,4,3,2,1,0:T(8,128)(2,1)}, bf16[8,5,32,192]{3,2,1,0:T(8,128)(2,1)}, bf16[8,5,32,192]{3,2,1,0:T(8,128)(2,1)}) custom-call(f32[2,4,224,384]{3,2,1,0:T(8,128)} %bitcast.42, bf16[8,5,32,192]{3,2,1,0:T(8,128)(2,1)} %bitcast.44, bf16[5,32,192]{2,1,0:T(8,128)(2,1)} %get-tuple-element.21.refs_2_), custom_call_target="tpu_custom_call" | custom-call | tf_op jit(solution)/shard_map/reduce/pallas_call | solution.py:526
  119.8 0.0 copy-done
  119.9 1.6 %dynamic-slice_bitcast_fusion.1 = (bf16[1,9,192,192]{3,2,1,0:T(8,128)(2,1)S(1)}, bf16[1,9,192,192]{3,2,1,0:T(8,128)(2,1)S(1)}) fusion(bf16[9,384,384]{2,1,0:T(8,128)(2,1)S(1)} %bitcast.41, s32[]{:T(128)S(6)} %select_n.13, s32[]{:T(128)S(6)} %select_n.15), kind=kLoop, calls=%fused_computation.2 | loop fusion | bytes 2654216 | tf_op jit(solution)/shard_map/stack | solution.py:498
  121.5 1.5 %pad_maximum_fusion.weight = bf16[2,9,192,192]{3,2,1,0:T(8,128)(2,1)} fusion(bf16[1,9,192,192]{3,2,1,0:T(8,128)(2,1)S(1)} %get-tuple-element.28, bf16[1,9,192,192]{3,2,1,0:T(8,128)(2,1)S(1)} %get-tuple-element.27), kind=kLoop, calls=%fused_computation | loop fusion | flops 663552 | bytes 2654208 | tf_op jit(solution)/shard_map/stack | solution.py:498
  123.0 10.9 %final.1 = (bf16[32,32,192]{2,1,0:T(8,128)(2,1)}, bf16[32,32,192]{2,1,0:T(8,128)(2,1)}) custom-call(s32[128,4]{1,0:T(8,128)} %copy.35.edge_tiles, s32[128,4]{1,0:T(8,128)} %copy.36.edge_turns, s32[128,4]{1,0:T(8,128)} %copy.37.corner_tiles, s32[128,4]{1,0:T(8,128)} %copy.38.corner_turns, f32[34,32,192]{2,1,0:T(8,128)} %get-tuple-element.17.interior, ...), custom_call_target="tpu_custom_call" | custom-call | tf_op jit(solution)/shard_map/final/pallas_call | solution.py:559
  133.9 0.0 copy-done.1
  133.9 0.1 slice.48
  134.1 0.1 slice.54
  134.2 1.8 %copy.39 = f32[2,9,96,384]{3,2,0,1:T(8,128)} copy(bf16[2,9,96,384]{3,2,1,0:T(8,128)(2,1)S(1)} %bitcast.39) | data formatting | bytes 3981312 | tf_op jit(solution)/shard_map/reshape | solution.py:570
  (10 shorter events, 0.1 us)
Async XLA Ops:
  56.9 63.0 %copy-start = (bf16[3,3,384,384]{3,2,1,0:T(8,128)(2,1)S(1)}, bf16[3,3,384,384]{3,2,1,0:T(8,128)(2,1)}, u32[]{:S(2)}) copy-start(bf16[3,3,384,384]{3,2,1,0:T(8,128)(2,1)} %param.8) | copy-start | bytes 7962628
  123.0 10.9 %copy-start.1 = (bf16[2,4,2,8,16,384]{5,4,3,2,1,0:T(8,128)(2,1)S(1)}, bf16[2,4,2,8,16,384]{5,4,3,2,1,0:T(8,128)(2,1)}, u32[]{:S(2)}) copy-start(bf16[2,4,2,8,16,384]{5,4,3,2,1,0:T(8,128)(2,1)} %get-tuple-element.26) | copy-start | bytes 4718596

commit v2 on v1

v2 whole, which is shorter than its diff:
```python
import math

import jax
import jax.numpy as jnp
import numpy as np
from jax import lax
from jax.experimental import pallas as pl
from jax.experimental.pallas import tpu as pltpu
from jax.sharding import PartitionSpec as P

MESH = pl.DeviceIdType.MESH
SPAN = 4
OFFSETS = [-4, -3, -2, -1, 1, 2, 3, 4]
S = 32
ROWS = S * S
UNIT = 16
VM = pltpu.VMEM
BF = jnp.bfloat16
F32 = jnp.float32


def turn_tables():
    labels = [[3 * row + col for col in range(3)] for row in range(3)]

    def turn_once(block):
        return [[block[col][2 - row] for col in range(3)] for row in range(3)]

    def sides_of(block):
        return [
            list(block[0]),
            [block[row][2] for row in range(3)],
            list(block[2]),
            [block[row][0] for row in range(3)],
        ]

    def corners_of(block):
        return [block[0][0], block[0][2], block[2][2], block[2][0]]

    base_sides = sides_of(labels)
    base_corners = corners_of(labels)
    edge_table = np.zeros((4, 4), np.int32)
    corner_table = np.zeros((4, 4), np.int32)
    for border in range(4):
        turned = labels
        for quarter in range(4):
            wanted = sides_of(turned)[(border + 2) % 4]
            for side_index in range(4):
                if base_sides[side_index] == wanted:
                    edge_table[border, quarter] = side_index
                if base_sides[side_index][::-1] == wanted:
                    edge_table[border, quarter] = side_index + 4
            corner_cell = corners_of(turned)[(border + 2) % 4]
            for corner_index in range(4):
                if base_corners[corner_index] == corner_cell:
                    corner_table[border, quarter] = corner_index
            turned = turn_once(turned)
    return (edge_table, corner_table)


EDGE_TABLE, CORNER_TABLE = turn_tables()


def lookup(table, border, turn):
    row = [int(v) for v in table[border]]
    value = jnp.int32(row[0])
    for quarter in range(1, 4):
        value = jnp.where(turn == quarter, jnp.int32(row[quarter]), value)
    return value


def slot_of(offset):
    return offset + SPAN if offset < 0 else offset + SPAN - 1


def wrap(index, size):
    return lax.rem(index + size, jnp.int32(size))


def coords():
    tile = lax.axis_index("tile")
    ch = lax.axis_index("ch")
    core = lax.rem(tile, 2)
    y = lax.rem(tile // 2, 4)
    xl = lax.rem(tile // 8, 2)
    z = tile // 16
    return tile, ch, core, y, xl, z


def dev(tile, ch):
    return {"tile": tile, "ch": ch}


def x_neighbours(tile, ch, xl):
    beside = tile + 8 - 16 * xl
    return dev(beside, ch), dev(beside, 1 - ch)


def remote(src, dst, send, recv, where):
    return pltpu.make_async_remote_copy(
        src_ref=src, dst_ref=dst, send_sem=send, recv_sem=recv, device_id=where, device_id_type=MESH
    )


class Swap:
    def __init__(self, src, dst, relay, sems, tile, ch, xl):
        self.n = relay.shape[1]
        near, far = x_neighbours(tile, ch, xl)
        self.first, self.second = [], []
        for i in range(self.n):
            for path in range(2):
                hop1, hop2 = (near, far) if path == 0 else (far, near)
                j = path * self.n + i
                self.first.append(remote(src.at[j], relay.at[path, i], sems.at[0, j], sems.at[1, j], hop1))
                self.second.append(remote(relay.at[path, i], dst.at[j], sems.at[2, j], sems.at[3, j], hop2))

    def start(self):
        for copy in self.first:
            copy.start()

    def relay(self):
        for one, two in zip(self.first, self.second):
            one.wait_recv()
            two.start()

    def finish_sends(self):
        for one, two in zip(self.first, self.second):
            one.wait_send()
            two.wait_send()


def near_copies(src, dst, sems, tile, ch, tiles):
    copies = []
    for offset in OFFSETS:
        k = slot_of(-offset)
        copies.append(
            remote(src, dst.at[k], sems.at[0, k], sems.at[1, k], dev(wrap(tile + offset, tiles), ch))
        )
    return copies


def iota2(shape, dim):
    return lax.broadcasted_iota(jnp.int32, shape, dim)


def source_slot(target, tile, tiles):
    away = wrap(target - tile, tiles)
    return jnp.clip(jnp.where(away > tiles // 2, away - tiles + SPAN, away + SPAN - 1), 0, 2 * SPAN - 1)


def spread_columns(buf, row, lanes, x, left, right):
    io = iota2(x.shape, 0)
    buf[1, row, :, lanes] = x.astype(BF)
    buf[0, row, :, lanes] = jnp.where(io == 0, left, pltpu.roll(x, 1, 0)).astype(BF)
    buf[2, row, :, lanes] = jnp.where(io == S - 1, right, pltpu.roll(x, S - 1, 0)).astype(BF)


def pack(x):
    return jnp.concatenate([x[: S // 2], x[S // 2 :]], axis=1)


def unpack(x):
    c = x.shape[1] // 2
    return jnp.concatenate([x[:, :c], x[:, c:]], axis=0)


def one_hot_rows(rows, target, width):
    return jnp.where(iota2((rows, width), 1) == target, 1.0, 0.0).astype(BF)


TN = (((0,), (0,)), ((), ()))
NT = (((1,), (1,)), ((), ()))


def fused_kernel(
    scale,
    edge_tiles_in, edge_turns_in, corner_tiles_in, corner_turns_in, feat_in, cot_in, weight_in,
    output, grad_features, gathered,
    edge_tiles, edge_turns, corner_tiles, corner_turns,
    feat, cot, weight, rows_weight, out_weight,
    lines, sides, all_sides, cot_packed, cot_other, relay_a,
    padded, columns, cots, cot_columns, grads, interior, pieces, all_pieces,
    packed, packed_other, relay_b, shifted, partial_out, hits, sums,
    pair_in, y_out, y_in, acc, x_in, z_out, z_in,
    load_sems, side_sems, swap_a_sems, swap_b_sems, piece_sems,
    pair_sems, y_sems, x_sems, z_sems, gz_sems, gx_sems, gy_sems, gp_sems,
):
    tiles = 128
    tile, ch, core, y, xl, z = coords()
    C2 = feat.shape[2]
    C = 2 * C2
    near, far = x_neighbours(tile, ch, xl)
    pair = dev(tile + 1 - 2 * core, ch)
    y_at = [lax.rem(y + 1 + j, 4) for j in range(3)]
    y_peer = [dev(tile + 2 * (q - y), ch) for q in y_at]
    z_at = [lax.rem(z + 1 + j, 8) for j in range(7)]
    z_peer = [dev(tile + 16 * (q - z), ch) for q in z_at]
    greeted = (
        [dev(wrap(tile + o, tiles), ch) for o in OFFSETS] + [near, far, pair] + y_peer + z_peer
    )
    ready = pltpu.get_barrier_semaphore()
    for where in greeted:
        pl.semaphore_signal(ready, inc=1, device_id=where, device_id_type=MESH)

    loads = [
        pltpu.make_async_copy(a, b, load_sems.at[i])
        for i, (a, b) in enumerate(
            (
                (feat_in, feat),
                (cot_in, cot),
                (edge_tiles_in, edge_tiles),
                (edge_turns_in, edge_turns),
                (corner_tiles_in, corner_tiles),
                (corner_turns_in, corner_turns),
                (weight_in, weight),
            )
        )
    ]
    for load in loads:
        load.start()

    loads[0].wait()

    def take_columns(row, carry):
        x = feat[row].astype(F32)
        lines[0, pl.ds(row, 1)] = x[0:1]
        lines[1, pl.ds(row, 1)] = x[S - 1 : S]
        return carry

    lax.fori_loop(0, S, take_columns, 0)
    sides[0] = pack(feat[0].astype(F32)).astype(BF)
    sides[1] = pack(lines[1]).astype(BF)
    sides[2] = pack(feat[S - 1].astype(F32)).astype(BF)
    sides[3] = pack(lines[0]).astype(BF)
    loads[1].wait()

    def pack_cot(row, carry):
        at = pl.multiple_of(lax.rem(row, 4) * 16, 16)
        cot_packed[row // 4, pl.ds(at, 16)] = pack(cot[row].astype(F32)).astype(BF)
        return carry

    lax.fori_loop(0, S, pack_cot, 0)
    pl.semaphore_wait(ready, len(greeted))
    swap_a = Swap(cot_packed, cot_other, relay_a, swap_a_sems, tile, ch, xl)
    swap_a.start()
    side_copies = near_copies(sides, all_sides, side_sems, tile, ch, tiles)
    for copy in side_copies:
        copy.start()

    zero = jnp.zeros((S, C), BF)
    for part in range(3):
        for row in (0, 1, S + 2, S + 3):
            cots[part, row] = zero
    cot_columns[...] = jnp.zeros_like(cot_columns)
    nothing = jnp.zeros((1, C2), F32)

    def shift_own(row, carry):
        x = cot[row].astype(F32)
        spread_columns(cots, row + 2, slice(0, C2), x, nothing, nothing)
        cot_columns[0, pl.ds(row + 2, 1), 0:C2] = x[0:1]
        cot_columns[1, pl.ds(row + 2, 1), 0:C2] = x[S - 1 : S]
        return carry

    lax.fori_loop(0, S, shift_own, 0)
    swap_a.relay()

    for i in range(2, 6):
        loads[i].wait()
    for copy in side_copies:
        copy.wait_recv()
    halos = []
    for border in range(4):
        source = source_slot(edge_tiles[tile, border], tile, tiles)
        slot = lookup(EDGE_TABLE, border, edge_turns[tile, border])
        rev = slot // 4
        x = unpack(all_sides[source, slot - 4 * rev].astype(F32)).astype(BF)
        ii = iota2((S, 1), 0)
        hot = one_hot_rows(S, jnp.where(rev == 1, S - 1 - ii, ii), S)
        halos.append(jnp.dot(hot, x, preferred_element_type=F32))
    columns[0, 1 : S + 1] = halos[3]
    columns[1, 1 : S + 1] = halos[1]
    for corner in range(4):
        source = source_slot(corner_tiles[tile, corner], tile, tiles)
        slot = lookup(CORNER_TABLE, corner, corner_turns[tile, corner])
        cells = all_sides[source, jnp.where(slot < 2, 0, 2)].astype(F32)
        first = (slot == 0) | (slot == 3)
        at = 0 if corner < 2 else S + 1
        columns[(0, 1, 1, 0)[corner], at : at + 1] = jnp.where(first, cells[0:1, :C2], cells[15:16, C2:])
    padded[1, 0] = halos[0].astype(BF)
    padded[1, S + 1] = halos[2].astype(BF)
    padded[1, 1 : S + 1] = feat[...]

    def shift_features(row, carry):
        x = padded[1, row].astype(F32)
        spread_columns(
            padded, row, slice(0, C2), x, columns[0, pl.ds(row, 1)], columns[1, pl.ds(row, 1)]
        )
        return carry

    lax.fori_loop(0, S + 2, shift_features, 0)
    for copy in swap_a.second:
        copy.wait_recv()

    def shift_other(row, carry):
        at = pl.multiple_of(lax.rem(row, 4) * 16, 16)
        x = unpack(cot_other[row // 4, pl.ds(at, 16)].astype(F32))
        spread_columns(cots, row + 2, slice(C2, C), x, nothing, nothing)
        cot_columns[0, pl.ds(row + 2, 1), C2:C] = x[0:1]
        cot_columns[1, pl.ds(row + 2, 1), C2:C] = x[S - 1 : S]
        return carry

    lax.fori_loop(0, S, shift_other, 0)

    def weight_grad(tap, carry):
        a, b = tap // 3, lax.rem(tap, 3)
        window = padded[b, pl.ds(a, S)].reshape(ROWS, C2)
        full = cots[1, 2 : S + 2].reshape(ROWS, C)
        part = lax.dot_general(window, full, TN, preferred_element_type=F32)
        at = pl.multiple_of(tap * (C2 // 2), 32)
        grads[0, pl.ds(at, C2 // 2)] = part[: C2 // 2]
        grads[1, pl.ds(at, C2 // 2)] = part[C2 // 2 :]
        return carry

    lax.fori_loop(0, 9, weight_grad, 0)
    tail = grads.shape[1] - 9 * (C2 // 2)
    grads[:, 9 * (C2 // 2) :] = jnp.zeros((2, tail, C), F32)

    chunk = 14 * UNIT
    order = y_at + [y]
    pair_copies = []
    for j, q in enumerate(order):
        src = grads.at[1 - core, pl.ds(pl.multiple_of(q * chunk, chunk), chunk)]
        pair_copies.append(remote(src, pair_in.at[j], pair_sems.at[0, j], pair_sems.at[1, j], pair))
        pair_copies[j].start()

    def pack_padded(row, carry):
        packed[row // 5, lax.rem(row, 5)] = pack(padded[1, row].astype(F32)).astype(BF)
        return carry

    lax.fori_loop(0, S + 2, pack_padded, 0)
    packed[6, 4] = pack(columns[0, 1 : S + 1]).astype(BF)
    packed[7, 0] = pack(columns[1, 1 : S + 1]).astype(BF)
    io = iota2((16, C), 0)
    ends = jnp.zeros((16, C), F32)
    for corner in range(4):
        at = 0 if corner < 2 else S + 1
        value = columns[(0, 1, 1, 0)[corner], at : at + 1]
        ends = jnp.where(io == corner, jnp.concatenate([value, value], axis=1), ends)
    packed[7, 1] = ends.astype(BF)
    for i in range(2, 5):
        packed[7, i] = jnp.zeros((16, C), BF)
    swap_b = Swap(packed, packed_other, relay_b, swap_b_sems, tile, ch, xl)

    y_copies = [
        remote(y_out.at[j], y_in.at[j], y_sems.at[0, j], y_sems.at[1, j], y_peer[j]) for j in range(3)
    ]
    for j in range(4):
        pair_copies[j].wait_recv()
        at = pl.multiple_of(order[j] * chunk, chunk)
        total = grads[core, pl.ds(at, chunk)] + pair_in[j]
        if j < 3:
            y_out[j] = total.astype(BF)
            y_copies[j].start()
        else:
            acc[...] = total.reshape(acc.shape)
    swap_b.start()

    loads[6].wait()

    def turn_weight(tap, carry):
        w = weight[tap, pl.ds(pl.multiple_of(ch * C2, 16), C2)].astype(F32)
        w = jnp.where(ch == 0, w, jnp.concatenate([w[:, C2:], w[:, :C2]], axis=1))
        rows_weight[tap] = w.astype(BF)
        for part in range(2):
            half = jnp.where(part == 0, ch, 1 - ch)
            w = weight[tap, pl.ds(pl.multiple_of(half * C2, 16), C2)].astype(F32)
            out_weight[part, tap] = jnp.where(ch == 0, w[:, :C2], w[:, C2:]).astype(BF)
        return carry

    lax.fori_loop(0, 9, turn_weight, 0)
    half = (S + 2) // 2

    def feature_grad(block, carry):
        total = None
        for a in range(3):
            for b in range(3):
                window = cots[2 - b, pl.ds(block * half + 2 - a, half)].reshape(half * S, C)
                term = lax.dot_general(window, rows_weight[3 * a + b], NT, preferred_element_type=F32)
                total = term if total is None else total + term
        interior[pl.ds(block * half, half)] = total.reshape(half, S, C2)
        return carry

    lax.fori_loop(0, 2, feature_grad, 0)
    pieces[0] = pack(interior[0]).astype(BF)
    pieces[2] = pack(interior[S + 1]).astype(BF)
    tips = []
    for side in range(2):
        total = None
        for a in range(3):
            line = cot_columns[side, 2 - a : 2 - a + 40].astype(BF)
            term = lax.dot_general(line, rows_weight[3 * a + 2 * side], NT, preferred_element_type=F32)
            total = term if total is None else total + term
        cot_columns[side, 0:40, 0:C2] = total
        pieces[3 - 2 * side] = pack(cot_columns[side, 1 : S + 1, 0:C2]).astype(BF)
        tips.append((total[0:1], total[S + 1 : S + 2]))
    io = iota2((16, C), 0)
    ends = jnp.zeros((16, C), F32)
    for corner, value in enumerate((tips[0][0], tips[1][0], tips[1][1], tips[0][1])):
        ends = jnp.where(io == corner, jnp.concatenate([value, value], axis=1), ends)
    pieces[4] = ends.astype(BF)
    piece_copies = near_copies(pieces, all_pieces, piece_sems, tile, ch, tiles)
    for copy in piece_copies:
        copy.start()
    swap_b.relay()

    for j in range(3):
        y_copies[j].wait_recv()
        acc[...] += y_in[j].astype(F32).reshape(acc.shape)
    x_copy = remote(acc.at[1 - xl], x_in, x_sems.at[0], x_sems.at[1], near)
    x_copy.start()
    z_out[7] = jnp.zeros(z_out.shape[1:], F32)
    x_copy.wait_recv()
    z_out[0:7] = (acc[xl] + x_in[...]).reshape(7, UNIT, C)
    z_copies = [
        remote(z_out.at[z_at[j]], z_in.at[j], z_sems.at[0, j], z_sems.at[1, j], z_peer[j])
        for j in range(7)
    ]
    for copy in z_copies:
        copy.start()

    rows = S // 2

    def convolve_own(block, carry):
        total = None
        for a in range(3):
            for b in range(3):
                window = padded[b, pl.ds(block * rows + a, rows)].reshape(rows * S, C2)
                term = jnp.dot(window, out_weight[0, 3 * a + b], preferred_element_type=F32)
                total = term if total is None else total + term
        partial_out[pl.ds(block * rows, rows)] = total.reshape(rows, S, C2)
        return carry

    lax.fori_loop(0, 2, convolve_own, 0)

    total = z_out[z]
    for j in range(7):
        z_copies[j].wait_recv()
        total = total + z_in[j]
    total = total * scale
    total = jnp.where(ch == 0, total, jnp.concatenate([total[:, C2:], total[:, :C2]], axis=1))
    gathered[core, y, xl, z] = total.astype(BF)
    spot = gathered.at[core, y, xl, z]
    gz_copies = [
        remote(spot, spot, gz_sems.at[0, j], gz_sems.at[1, j], z_peer[j]) for j in range(7)
    ]
    for copy in gz_copies:
        copy.start()

    for copy in swap_b.second:
        copy.wait_recv()
    left_line = unpack(packed_other[6, 4].astype(F32))
    right_line = unpack(packed_other[7, 0].astype(F32))
    ends = packed_other[7, 1].astype(F32)
    columns[0, 1 : S + 1] = left_line
    columns[1, 1 : S + 1] = right_line
    for corner in range(4):
        at = 0 if corner < 2 else S + 1
        columns[(0, 1, 1, 0)[corner], at : at + 1] = ends[corner : corner + 1, :C2]

    def shift_partner(row, carry):
        x = unpack(packed_other[row // 5, lax.rem(row, 5)].astype(F32))
        spread_columns(
            shifted, row, slice(0, C2), x, columns[0, pl.ds(row, 1)], columns[1, pl.ds(row, 1)]
        )
        return carry

    lax.fori_loop(0, S + 2, shift_partner, 0)
    for copy in gz_copies:
        copy.wait_recv()
    spot = gathered.at[core, y, xl]
    gx_copy = remote(spot, spot, gx_sems.at[0], gx_sems.at[1], near)
    gx_copy.start()

    for copy in piece_copies:
        copy.wait_recv()
    for offset in OFFSETS:
        k = slot_of(-offset)
        source = wrap(tile - offset, tiles)
        for border in range(4):
            hit = edge_tiles[source, border] == tile
            slot = lookup(EDGE_TABLE, border, edge_turns[source, border])
            rev = slot // 4
            ii = iota2((S, 1), 0)
            target = jnp.where(rev == 1, S - 1 - ii, ii) + (slot - 4 * rev) * S
            hot = one_hot_rows(S, jnp.where(hit, target, -1), 4 * S)
            hits[0, k, border] = hot[:16]
            hits[1, k, border] = hot[16:]
        ii = iota2((16, 1), 0)
        target = jnp.full((16, 1), -1, jnp.int32)
        for corner in range(4):
            hit = corner_tiles[source, corner] == tile
            slot = lookup(CORNER_TABLE, corner, corner_turns[source, corner])
            cell = jnp.where(slot < 2, 0, 2 * S) + jnp.where((slot == 0) | (slot == 3), 0, S - 1)
            target = jnp.where((ii == corner) & hit, cell, target)
        hits[0, k, 4] = one_hot_rows(16, target, 4 * S)
        hits[1, k, 4] = jnp.zeros((16, 4 * S), BF)
    flat = all_pieces[...].reshape(8 * 5 * 16, C)
    parts = [
        lax.dot_general(hits[i].reshape(8 * 5 * 16, 4 * S), flat, TN, preferred_element_type=F32)
        for i in range(2)
    ]
    sums[...] = (parts[0][:, :C2] + parts[1][:, C2:]).reshape(4, S, C2)
    gx_copy.wait_recv()
    spot = gathered.at[core, y]
    gy_copies = [remote(spot, spot, gy_sems.at[0, j], gy_sems.at[1, j], y_peer[j]) for j in range(3)]
    for copy in gy_copies:
        copy.start()
    gp_copies = []
    for j in range(4):
        q = y if j == 0 else lax.rem(y + 4 - j, 4)
        spot = gathered.at[core, q]
        gp_copies.append(remote(spot, spot, gp_sems.at[0, j], gp_sems.at[1, j], pair))
    gp_copies[0].start()

    def add_sides(row, carry):
        io = iota2((S, C2), 0)
        x = interior[row + 1]
        x = x + jnp.where(io == 0, sums[3, pl.ds(row, 1)], 0.0)
        x = x + jnp.where(io == S - 1, sums[1, pl.ds(row, 1)], 0.0)
        x = x + jnp.where(row == 0, sums[0], 0.0)
        x = x + jnp.where(row == S - 1, sums[2], 0.0)
        grad_features[row] = x.astype(BF)
        return carry

    lax.fori_loop(0, S, add_sides, 0)

    def convolve_other(block, carry):
        total = partial_out[pl.ds(block * rows, rows)].reshape(rows * S, C2)
        for a in range(3):
            for b in range(3):
                window = shifted[b, pl.ds(block * rows + a, rows)].reshape(rows * S, C2)
                total = total + jnp.dot(window, out_weight[1, 3 * a + b], preferred_element_type=F32)
        output[pl.ds(block * rows, rows)] = total.reshape(rows, S, C2).astype(BF)
        return carry

    lax.fori_loop(0, 2, convolve_other, 0)

    for j in range(3):
        gy_copies[j].wait_recv()
        gp_copies[j + 1].start()
    swap_a.finish_sends()
    swap_b.finish_sends()
    for copy in gp_copies:
        copy.wait()
    x_copy.wait_send()
    gx_copy.wait_send()
    for copy in side_copies + piece_copies + pair_copies + y_copies + z_copies + gz_copies + gy_copies:
        copy.wait_send()


VSPEC = pl.BlockSpec(memory_space=VM)
ANY = pl.BlockSpec(memory_space=pl.ANY)
DMA = pltpu.SemaphoreType.DMA
SM = pltpu.SMEM


def body(features, weight, cotangent, edge_tiles, edge_turns, corner_tiles, corner_turns):
    field = features[0]
    C2 = field.shape[2]
    C = 2 * C2
    shape = jax.ShapeDtypeStruct
    table = SM((128, 4), jnp.int32)
    output, grad_features, gathered = pl.pallas_call(
        lambda *refs: fused_kernel(1.0 / math.sqrt(128 * ROWS), *refs),
        name="fused",
        out_shape=(
            shape((S, S, C2), BF),
            shape((S, S, C2), BF),
            shape((2, 4, 2, 8, UNIT, C), BF),
        ),
        in_specs=[ANY] * 7,
        out_specs=(VSPEC,) * 3,
        scratch_shapes=[
            table, table, table, table,
            VM((S, S, C2), BF),
            VM((S, S, C2), BF),
            VM((9, C, C), BF),
            VM((9, C2, C), BF),
            VM((2, 9, C2, C2), BF),
            VM((2, S, C2), F32),
            VM((4, 16, C), BF),
            VM((8, 4, 16, C), BF),
            VM((8, 64, C), BF),
            VM((8, 64, C), BF),
            VM((2, 4, 64, C), BF),
            VM((3, S + 2, S, C2), BF),
            VM((2, 40, C2), F32),
            VM((3, S + 4, S, C), BF),
            VM((2, 48, C), F32),
            VM((2, 56 * UNIT, C), F32),
            VM((S + 2, S, C2), F32),
            VM((5, 16, C), BF),
            VM((8, 5, 16, C), BF),
            VM((8, 5, 16, C), BF),
            VM((8, 5, 16, C), BF),
            VM((2, 4, 5, 16, C), BF),
            VM((3, S + 2, S, C2), BF),
            VM((S, S, C2), F32),
            VM((2, 8, 5, 16, 4 * S), BF),
            VM((4, S, C2), F32),
            VM((4, 14 * UNIT, C), F32),
            VM((3, 14 * UNIT, C), BF),
            VM((3, 14 * UNIT, C), BF),
            VM((2, 7 * UNIT, C), F32),
            VM((7 * UNIT, C), F32),
            VM((8, UNIT, C), F32),
            VM((7, UNIT, C), F32),
            DMA((7,)),
            DMA((2, 8)),
            DMA((4, 8)),
            DMA((4, 8)),
            DMA((2, 8)),
            DMA((2, 4)),
            DMA((2, 3)),
            DMA((2,)),
            DMA((2, 7)),
            DMA((2, 7)),
            DMA((2,)),
            DMA((2, 3)),
            DMA((2, 4)),
        ],
        compiler_params=pltpu.CompilerParams(
            vmem_limit_bytes=60 * 1024 * 1024, collective_id=0, has_side_effects=True
        ),
    )(edge_tiles, edge_turns, corner_tiles, corner_turns, field, cotangent[0], weight.reshape(9, C, C))

    flat = gathered[:, :, :, :7].reshape(2, 56 * UNIT, C)[:, : 9 * (C2 // 2)]
    grad_weight = flat.reshape(2, 9, C2 // 2, C).transpose(1, 0, 2, 3).astype(F32).reshape(3, 3, C2, C)
    return (output[None], grad_features[None], grad_weight)


def solution(mesh):
    return jax.shard_map(
        body,
        mesh=mesh,
        in_specs=(
            P("tile", None, None, "ch"),
            P(),
            P("tile", None, None, "ch"),
            P(),
            P(),
            P(),
            P(),
        ),
        out_specs=(
            P("tile", None, None, "ch"),
            P("tile", None, None, "ch"),
            P(None, None, "ch", None),
        ),
        check_vma=False,
    )
```

time: 137 us -> 96.6 us (0.71)
  Pallas kernels: 116 us -> 84.4 us
  local copies, waits for them, and re-layouts: 15.5 us -> 10.7 us
  other arithmetic: 4.09 us -> 0 us
    pallas_call x4 -> x1, Pallas kernels: 116 us -> 84.4 us  [body(): pl.pallas_call(lambda *refs: fused_kernel(1.0 / math.sqrt(128 * ROWS), *r...]
    another operation x3 -> x0, other arithmetic: 3.09 us -> none  [the longest x1 1.55 us: body(): jnp.stack([lax.dynamic_slice_in_dim(out_columns, ch * C2, C2, 1), lax.dyn...]
    dynamic_slice x1 -> x0, local copies, waits for them, and re-layouts: 2.53 us -> none  [body(): weight_rows = lax.dynamic_slice_in_dim(taps, ch * C2, C2, 1)]
    slice x5 -> x0, local copies, waits for them, and re-layouts: 2.5 us -> none  [the longest x2 1.76 us: body(): sides = jnp.stack([field[0], field[:, -1], field[-1], field[:, 0]])]
    unnamed x11 -> x10, local copies, waits for them, and re-layouts: 5.63 us -> 7.26 us
    another operation x1 -> x0, local copies, waits for them, and re-layouts: 1.61 us -> none  [body(): jnp.stack([lax.dynamic_slice_in_dim(out_columns, ch * C2, C2, 1), lax.dyn...]
where the time goes in v2:
time: 96.6 us; the launch traced here: 95.7 us
  Pallas kernels  84.4 us (87%)
  local copies, waits for them, and re-layouts  10.7 us (11%)
    pallas_call x1, Pallas kernels, body(): pl.pallas_call(lambda *refs: fused_kernel(1.0 / math.sqrt(128 * ROWS), *r...  84.4 us
    unnamed x10, local copies, waits for them, and re-layouts  7.26 us

profile of v2, /device:TPU:1, one launch (start us, length us, event | category | flops | bytes accessed | tf_op | source)
XLA Modules:
  0.0 95.7 jit_solution(2648073740387636602)
XLA Ops:
  0.6 1.4 %copy.10.refs_0_ = s32[128,4]{1,0:T(8,128)} copy(s32[128,4]{0,1:T(4,128)} %param.10) | data formatting | bytes 4096 | tf_op args[3]
  2.0 1.4 %copy.11.refs_1_ = s32[128,4]{1,0:T(8,128)} copy(s32[128,4]{0,1:T(4,128)} %param.11) | data formatting | bytes 4096 | tf_op args[4]
  3.5 1.4 %copy.12.refs_2_ = s32[128,4]{1,0:T(8,128)} copy(s32[128,4]{0,1:T(4,128)} %param.12) | data formatting | bytes 4096 | tf_op args[5]
  4.9 1.4 %copy.13.refs_3_ = s32[128,4]{1,0:T(8,128)} copy(s32[128,4]{0,1:T(4,128)} %param.13) | data formatting | bytes 4096 | tf_op args[6]
  6.3 84.4 %fused.1 = (bf16[32,32,192]{2,1,0:T(8,128)(2,1)}, bf16[32,32,192]{2,1,0:T(8,128)(2,1)}, bf16[2,4,2,8,16,384]{5,4,3,2,1,0:T(8,128)(2,1)}) custom-call(s32[128,4]{1,0:T(8,128)} %copy.10.refs_0_, s32[128,4]{1,0:T(8,128)} %copy.11.refs_1_, s32[128,4]{1,0:T(8,128)} %copy.12.refs_2_, s32[128,4]{1,0:T(8,128)} %copy.13.refs_3_, bf16[32,32,192]{2,1,0:T(8,128)(2,1)} %bitcast.15, ...), custom_call_target="tpu_custom_call" | custom-call | tf_op jit(solution)/shard_map/fused/pallas_call | solution.py:572
  90.7 1.5 %slice.6 = bf16[2,4,2,7,16,384]{5,4,3,2,1,0:T(8,128)(2,1)S(1)} slice(bf16[2,4,2,8,16,384]{5,4,3,2,1,0:T(8,128)(2,1)} %get-tuple-element.8), slice={[0:2], [0:4], [0:2], [0:7], [0:16], [0:384]} | slice | bytes 2752512 | tf_op jit(solution)/shard_map/slice | solution.py:636
  92.2 0.1 slice.8
  92.3 0.0 copy-start.1
  92.3 0.0 copy-start
  92.3 1.8 %copy.14 = f32[2,9,96,384]{3,2,0,1:T(8,128)} copy(bf16[2,9,96,384]{3,2,1,0:T(8,128)(2,1)S(1)} %bitcast.12) | data formatting | bytes 3981312 | tf_op jit(solution)/shard_map/reshape | solution.py:637
  94.1 0.0 copy-done.1
  94.1 0.8 copy.17
  94.9 0.0 copy-done
  94.9 0.8 copy.18
Async XLA Ops:
  92.3 1.8 %copy-start.1 = (bf16[32,32,192]{2,1,0:T(8,128)(2,1)S(1)}, bf16[32,32,192]{2,1,0:T(8,128)(2,1)}, u32[]{:S(2)}) copy-start(bf16[32,32,192]{2,1,0:T(8,128)(2,1)} %get-tuple-element.6) | copy-start | bytes 1179652
  92.3 2.6 %copy-start = (bf16[32,32,192]{2,1,0:T(8,128)(2,1)S(1)}, bf16[32,32,192]{2,1,0:T(8,128)(2,1)}, u32[]{:S(2)}) copy-start(bf16[32,32,192]{2,1,0:T(8,128)(2,1)} %get-tuple-element.7) | copy-start | bytes 1179652

commit v3 on v2

v3 whole, which is shorter than its diff:
```python
import math

import jax
import jax.numpy as jnp
import numpy as np
from jax import lax
from jax.experimental import pallas as pl
from jax.experimental.pallas import tpu as pltpu
from jax.sharding import PartitionSpec as P

MESH = pl.DeviceIdType.MESH
SPAN = 4
OFFSETS = [-4, -3, -2, -1, 1, 2, 3, 4]
S = 32
ROWS = S * S
UNIT = 16
VM = pltpu.VMEM
BF = jnp.bfloat16
F32 = jnp.float32


def turn_tables():
    labels = [[3 * row + col for col in range(3)] for row in range(3)]

    def turn_once(block):
        return [[block[col][2 - row] for col in range(3)] for row in range(3)]

    def sides_of(block):
        return [
            list(block[0]),
            [block[row][2] for row in range(3)],
            list(block[2]),
            [block[row][0] for row in range(3)],
        ]

    def corners_of(block):
        return [block[0][0], block[0][2], block[2][2], block[2][0]]

    base_sides = sides_of(labels)
    base_corners = corners_of(labels)
    edge_table = np.zeros((4, 4), np.int32)
    corner_table = np.zeros((4, 4), np.int32)
    for border in range(4):
        turned = labels
        for quarter in range(4):
            wanted = sides_of(turned)[(border + 2) % 4]
            for side_index in range(4):
                if base_sides[side_index] == wanted:
                    edge_table[border, quarter] = side_index
                if base_sides[side_index][::-1] == wanted:
                    edge_table[border, quarter] = side_index + 4
            corner_cell = corners_of(turned)[(border + 2) % 4]
            for corner_index in range(4):
                if base_corners[corner_index] == corner_cell:
                    corner_table[border, quarter] = corner_index
            turned = turn_once(turned)
    return (edge_table, corner_table)


EDGE_TABLE, CORNER_TABLE = turn_tables()


def lookup(table, border, turn):
    row = [int(v) for v in table[border]]
    value = jnp.int32(row[0])
    for quarter in range(1, 4):
        value = jnp.where(turn == quarter, jnp.int32(row[quarter]), value)
    return value


def slot_of(offset):
    return offset + SPAN if offset < 0 else offset + SPAN - 1


def wrap(index, size):
    return lax.rem(index + size, jnp.int32(size))


def coords():
    tile = lax.axis_index("tile")
    ch = lax.axis_index("ch")
    core = lax.rem(tile, 2)
    y = lax.rem(tile // 2, 4)
    xl = lax.rem(tile // 8, 2)
    z = tile // 16
    return tile, ch, core, y, xl, z


def dev(tile, ch):
    return {"tile": tile, "ch": ch}


def x_neighbours(tile, ch, xl):
    beside = tile + 8 - 16 * xl
    return dev(beside, ch), dev(beside, 1 - ch)


def remote(src, dst, send, recv, where):
    return pltpu.make_async_remote_copy(
        src_ref=src, dst_ref=dst, send_sem=send, recv_sem=recv, device_id=where, device_id_type=MESH
    )


class Swap:
    def __init__(self, src, dst, relay, sems, tile, ch, xl):
        self.n = relay.shape[1]
        near, far = x_neighbours(tile, ch, xl)
        self.first, self.second = [], []
        for i in range(self.n):
            for path in range(2):
                hop1, hop2 = (near, far) if path == 0 else (far, near)
                j = path * self.n + i
                self.first.append(remote(src.at[j], relay.at[path, i], sems.at[0, j], sems.at[1, j], hop1))
                self.second.append(remote(relay.at[path, i], dst.at[j], sems.at[2, j], sems.at[3, j], hop2))

    def start(self):
        for copy in self.first:
            copy.start()

    def relay(self):
        for one, two in zip(self.first, self.second):
            one.wait_recv()
            two.start()

    def finish_sends(self):
        for one, two in zip(self.first, self.second):
            one.wait_send()
            two.wait_send()


def near_copies(src, dst, sems, tile, ch, tiles):
    copies = []
    for offset in OFFSETS:
        k = slot_of(-offset)
        copies.append(
            remote(src, dst.at[k], sems.at[0, k], sems.at[1, k], dev(wrap(tile + offset, tiles), ch))
        )
    return copies


def iota2(shape, dim):
    return lax.broadcasted_iota(jnp.int32, shape, dim)


def source_slot(target, tile, tiles):
    away = wrap(target - tile, tiles)
    return jnp.clip(jnp.where(away > tiles // 2, away - tiles + SPAN, away + SPAN - 1), 0, 2 * SPAN - 1)


def spread_columns(buf, row, lanes, x, left, right):
    io = iota2(x.shape, 0)
    buf[1, row, :, lanes] = x.astype(BF)
    buf[0, row, :, lanes] = jnp.where(io == 0, left, pltpu.roll(x, 1, 0)).astype(BF)
    buf[2, row, :, lanes] = jnp.where(io == S - 1, right, pltpu.roll(x, S - 1, 0)).astype(BF)


def pack(x):
    n = x.shape[0] // 2
    return jnp.concatenate([x[:n, :128], x[n:, :128], x[:n, 128:], x[n:, 128:]], axis=1)


def unpack(x):
    low = jnp.concatenate([x[:, :128], x[:, 256:320]], axis=1)
    high = jnp.concatenate([x[:, 128:256], x[:, 320:]], axis=1)
    return jnp.concatenate([low, high], axis=0)


def one_hot_rows(rows, target, width):
    return jnp.where(iota2((rows, width), 1) == target, 1.0, 0.0).astype(BF)


TN = (((0,), (0,)), ((), ()))
NT = (((1,), (1,)), ((), ()))
CHUNK = 14 * UNIT


class Reduce:
    def __init__(self, scale, bufs, sems, place):
        self.grads, self.pair_in, self.y_out, self.y_in, self.acc, self.x_in, self.z_out, self.z_in, self.gathered = bufs
        self.scale = scale
        tile, ch, core, y, xl, z = self.place = place
        self.near, _ = x_neighbours(tile, ch, xl)
        self.pair = dev(tile + 1 - 2 * core, ch)
        self.y_at = [lax.rem(y + 1 + j, 4) for j in range(3)]
        self.y_peer = [dev(tile + 2 * (q - y), ch) for q in self.y_at]
        self.z_at = [lax.rem(z + 1 + j, 8) for j in range(7)]
        self.z_from = [lax.rem(z + 7 - j, 8) for j in range(7)]
        self.z_peer = [dev(tile + 16 * (q - z), ch) for q in self.z_at]
        self.order = self.y_at + [y]
        pair_sems, y_sems, x_sems, z_sems, gz_sems, gx_sems, gy_sems, gp_sems = sems
        self.pair_copies = []
        for j, q in enumerate(self.order):
            part = self.grads.at[1 - core, pl.ds(pl.multiple_of(q * CHUNK, CHUNK), CHUNK)]
            self.pair_copies.append(
                remote(part, self.pair_in.at[j], pair_sems.at[0, j], pair_sems.at[1, j], self.pair)
            )
        self.y_copies = [
            remote(self.y_out.at[j], self.y_in.at[j], y_sems.at[0, j], y_sems.at[1, j], self.y_peer[j])
            for j in range(3)
        ]
        self.x_copy = remote(self.acc.at[1 - xl], self.x_in, x_sems.at[0], x_sems.at[1], self.near)
        own = jnp.minimum(z, 6)
        self.z_copies, self.gz_copies = [], []
        for j in range(7):
            part = self.z_out.at[jnp.minimum(self.z_at[j], 6)]
            self.z_copies.append(remote(part, self.z_in.at[j], z_sems.at[0, j], z_sems.at[1, j], self.z_peer[j]))
            spot = self.gathered.at[core, y, xl, own]
            self.gz_copies.append(remote(spot, spot, gz_sems.at[0, j], gz_sems.at[1, j], self.z_peer[j]))
        spot = self.gathered.at[core, y, xl]
        self.gx_copy = remote(spot, spot, gx_sems.at[0], gx_sems.at[1], self.near)
        self.gy_copies, self.gp_copies = [], []
        for k in range(2):
            half = xl if k == 0 else 1 - xl
            spot = self.gathered.at[core, y, half]
            for j in range(3):
                self.gy_copies.append(
                    remote(spot, spot, gy_sems.at[0, k, j], gy_sems.at[1, k, j], self.y_peer[j])
                )
            for j in range(4):
                q = y if j == 0 else lax.rem(y + 4 - j, 4)
                spot = self.gathered.at[core, q, half]
                self.gp_copies.append(remote(spot, spot, gp_sems.at[0, k, j], gp_sems.at[1, k, j], self.pair))

    def start(self):
        for copy in self.pair_copies:
            copy.start()

    def to_y(self):
        core = self.place[2]
        for j in range(4):
            self.pair_copies[j].wait_recv()
            at = pl.multiple_of(self.order[j] * CHUNK, CHUNK)
            total = self.grads[core, pl.ds(at, CHUNK)] + self.pair_in[j]
            if j < 3:
                self.y_out[j] = total.astype(BF)
                self.y_copies[j].start()
            else:
                self.acc[...] = total.reshape(self.acc.shape)

    def to_x(self):
        for j in range(3):
            self.y_copies[j].wait_recv()
            self.acc[...] += self.y_in[j].astype(F32).reshape(self.acc.shape)
        self.x_copy.start()

    def to_z(self):
        xl, z = self.place[4:]
        self.x_copy.wait_recv()
        self.z_out[...] = (self.acc[xl] + self.x_in[...]).reshape(self.z_out.shape)
        for j in range(7):
            pl.when(self.z_at[j] != 7)(self.z_copies[j].start)

    def to_gz(self):
        tile, ch, core, y, xl, z = self.place

        @pl.when(z != 7)
        def _():
            own = jnp.minimum(z, 6)
            total = self.z_out[own]
            for j in range(7):
                self.z_copies[j].wait_recv()
                total = total + self.z_in[j]
            self.gathered[core, y, xl, own] = (total * self.scale).astype(BF)
            for copy in self.gz_copies:
                copy.start()

    def to_gx(self):
        for j in range(7):
            pl.when(self.z_from[j] != 7)(self.gz_copies[j].wait_recv)
        self.gx_copy.start()
        for copy in self.gy_copies[:3]:
            copy.start()
        self.gp_copies[0].start()

    def to_gy(self):
        self.gx_copy.wait_recv()
        for copy in self.gy_copies[3:]:
            copy.start()
        self.gp_copies[4].start()

    def to_pair(self):
        for k in range(2):
            for j in range(3):
                self.gy_copies[3 * k + j].wait_recv()
                self.gp_copies[4 * k + j + 1].start()

    def finish(self):
        z = self.place[5]
        for copy in self.gp_copies:
            copy.wait()
        for copy in self.pair_copies + self.y_copies + [self.x_copy, self.gx_copy] + self.gy_copies:
            copy.wait_send()
        for j in range(7):
            pl.when(self.z_at[j] != 7)(self.z_copies[j].wait_send)
            pl.when(z != 7)(self.gz_copies[j].wait_send)


def fused_kernel(
    scale,
    edge_tiles_in, edge_turns_in, corner_tiles_in, corner_turns_in, feat_in, cot_in, weight_in,
    output, grad_features, gathered_1, gathered_2,
    edge_tiles, edge_turns, corner_tiles, corner_turns,
    feat, cot, weight, rows_weight, out_weight,
    lines, sides, all_sides, cot_packed, cot_other, relay_a,
    padded, columns, cots, cot_columns, interior, pieces, all_pieces,
    packed, packed_other, relay_b, shifted, partial_out, hits, sums,
    load_sems, side_sems, swap_a_sems, swap_b_sems, piece_sems,
    *streams,
):
    tiles = 128
    place = tile, ch, core, y, xl, z = coords()
    C2 = feat.shape[2]
    C = 2 * C2
    near, far = x_neighbours(tile, ch, xl)
    bufs = len(REDUCE_BUFS)
    sems = len(REDUCE_SEMS)
    first = Reduce(scale, streams[:bufs] + (gathered_1,), streams[bufs : bufs + sems], place)
    streams = streams[bufs + sems :]
    second = Reduce(scale, streams[:bufs] + (gathered_2,), streams[bufs:], place)
    greeted = [dev(wrap(tile + o, tiles), ch) for o in OFFSETS] + [near, far, first.pair]
    greeted = greeted + first.y_peer + first.z_peer
    ready = pltpu.get_barrier_semaphore()
    for where in greeted:
        pl.semaphore_signal(ready, inc=1, device_id=where, device_id_type=MESH)

    own_rows = pl.ds(pl.multiple_of(ch * C2, 64), C2)
    loads = [
        pltpu.make_async_copy(a, b, load_sems.at[i])
        for i, (a, b) in enumerate(
            (
                (feat_in, feat),
                (cot_in, cot),
                (edge_tiles_in, edge_tiles),
                (edge_turns_in, edge_turns),
                (corner_tiles_in, corner_tiles),
                (corner_turns_in, corner_turns),
                (weight_in, weight),
                (weight_in.at[:, own_rows], rows_weight),
            )
        )
    ]
    for load in loads:
        load.start()

    loads[0].wait()

    def take_columns(row, carry):
        x = feat[row].astype(F32)
        lines[0, pl.ds(row, 1)] = x[0:1]
        lines[1, pl.ds(row, 1)] = x[S - 1 : S]
        return carry

    lax.fori_loop(0, S, take_columns, 0, unroll=4)
    sides[0] = pack(feat[0])
    sides[1] = pack(lines[1].astype(BF))
    sides[2] = pack(feat[S - 1])
    sides[3] = pack(lines[0].astype(BF))
    loads[1].wait()

    def pack_cot(row, carry):
        for i in range(4):
            cot_packed[row, 16 * i : 16 * i + 16] = pack(cot[4 * row + i])
        return carry

    lax.fori_loop(0, S // 4, pack_cot, 0)
    pl.semaphore_wait(ready, len(greeted))
    swap_a = Swap(cot_packed, cot_other, relay_a, swap_a_sems, tile, ch, xl)
    swap_a.start()
    side_copies = near_copies(sides, all_sides, side_sems, tile, ch, tiles)
    for copy in side_copies:
        copy.start()

    zero = jnp.zeros((S, C), BF)
    for part in range(3):
        for row in (0, 1, S + 2, S + 3):
            cots[part, row] = zero
    cot_columns[...] = jnp.zeros_like(cot_columns)
    nothing = jnp.zeros((1, C2), F32)

    def fill(read, lanes):
        def shift(row, carry):
            x = read(row).astype(F32)
            spread_columns(cots, row + 2, lanes, x, nothing, nothing)
            cot_columns[0, pl.ds(row + 2, 1), lanes] = x[0:1]
            cot_columns[1, pl.ds(row + 2, 1), lanes] = x[S - 1 : S]
            return carry

        lax.fori_loop(0, S, shift, 0, unroll=4)

    def read_other(row):
        at = pl.multiple_of(lax.rem(row, 4) * 16, 16)
        return unpack(cot_other[row // 4, pl.ds(at, 16)])

    pl.when(ch == 0)(lambda: fill(lambda row: cot[row], slice(0, C2)))
    pl.when(ch == 1)(lambda: fill(lambda row: cot[row], slice(C2, C)))
    swap_a.relay()

    for i in range(2, 6):
        loads[i].wait()
    for copy in side_copies:
        copy.wait_recv()
    halos = []
    for border in range(4):
        source = source_slot(edge_tiles[border, tile], tile, tiles)
        slot = lookup(EDGE_TABLE, border, edge_turns[border, tile])
        rev = slot // 4
        x = unpack(all_sides[source, slot - 4 * rev])
        ii = iota2((S, 1), 0)
        hot = one_hot_rows(S, jnp.where(rev == 1, S - 1 - ii, ii), S)
        halos.append(jnp.dot(hot, x, preferred_element_type=F32))
    columns[0, 1 : S + 1] = halos[3]
    columns[1, 1 : S + 1] = halos[1]
    for corner in range(4):
        source = source_slot(corner_tiles[corner, tile], tile, tiles)
        slot = lookup(CORNER_TABLE, corner, corner_turns[corner, tile])
        cells = unpack(all_sides[source, jnp.where(slot < 2, 0, 2)]).astype(F32)
        start = (slot == 0) | (slot == 3)
        at = 0 if corner < 2 else S + 1
        columns[(0, 1, 1, 0)[corner], at : at + 1] = jnp.where(start, cells[0:1], cells[S - 1 : S])
    padded[1, 0] = halos[0].astype(BF)
    padded[1, S + 1] = halos[2].astype(BF)
    padded[1, 1 : S + 1] = feat[...]

    def shift_features(row, carry):
        packed[row // 5, lax.rem(row, 5)] = pack(padded[1, row])
        x = padded[1, row].astype(F32)
        spread_columns(
            padded, row, slice(0, C2), x, columns[0, pl.ds(row, 1)], columns[1, pl.ds(row, 1)]
        )
        return carry

    lax.fori_loop(0, S + 2, shift_features, 0, unroll=2)
    packed[6, 4] = pack(columns[0, 1 : S + 1].astype(BF))
    packed[7, 0] = pack(columns[1, 1 : S + 1].astype(BF))
    io = iota2((16, C2), 0)
    ends = jnp.zeros((16, C2), F32)
    for corner in range(4):
        at = 0 if corner < 2 else S + 1
        ends = jnp.where(io == corner, columns[(0, 1, 1, 0)[corner], at : at + 1], ends)
    packed[7, 1] = pack(jnp.concatenate([ends, ends], axis=0).astype(BF))
    for i in range(2, 5):
        packed[7, i] = jnp.zeros((16, C), BF)
    swap_b = Swap(packed, packed_other, relay_b, swap_b_sems, tile, ch, xl)
    swap_b.start()

    def weight_grad(stream, at):
        width = stream.grads.shape[2]
        lanes = pl.ds(pl.multiple_of(at, 128), width)
        block = C2 // 2

        def one_tap(tap, carry):
            a, b = tap // 3, lax.rem(tap, 3)
            window = padded[b, pl.ds(a, S)].reshape(ROWS, C2)
            full = cots[1, 2 : S + 2, :, lanes].reshape(ROWS, width)
            part = lax.dot_general(window, full, TN, preferred_element_type=F32)
            for i in range(2):
                index = 2 * tap + i
                half = index // 9
                spot = pl.multiple_of((index - 9 * half) * block, 32)
                stream.grads[half, pl.ds(spot, block)] = part[i * block : (i + 1) * block]
            return carry

        lax.fori_loop(0, 9, one_tap, 0)
        filled = 9 * block
        stream.grads[:, filled:] = jnp.zeros((2, stream.grads.shape[1] - filled, width), F32)

    weight_grad(first, 256 * ch)
    first.start()
    first.to_y()
    for copy in swap_a.second:
        copy.wait_recv()
    pl.when(ch == 0)(lambda: fill(read_other, slice(C2, C)))
    pl.when(ch == 1)(lambda: fill(read_other, slice(0, C2)))
    weight_grad(second, 128 - 128 * ch)
    second.start()
    swap_b.relay()
    second.to_y()
    first.to_x()

    loads[7].wait()
    half = (S + 2) // 2

    def feature_grad(block, carry):
        total = None
        for a in range(3):
            for b in range(3):
                window = cots[2 - b, pl.ds(block * half + 2 - a, half)].reshape(half * S, C)
                term = lax.dot_general(window, rows_weight[3 * a + b], NT, preferred_element_type=F32)
                total = term if total is None else total + term
        interior[pl.ds(block * half, half)] = total.reshape(half, S, C2)
        return carry

    lax.fori_loop(0, 2, feature_grad, 0)
    first.to_z()
    pieces[0] = pack(interior[0].astype(BF))
    pieces[2] = pack(interior[S + 1].astype(BF))
    tips = []
    for side in range(2):
        total = None
        for a in range(3):
            line = cot_columns[side, 2 - a : 2 - a + 40].astype(BF)
            term = lax.dot_general(line, rows_weight[3 * a + 2 * side], NT, preferred_element_type=F32)
            total = term if total is None else total + term
        cot_columns[side, 0:40, 0:C2] = total
        pieces[3 - 2 * side] = pack(cot_columns[side, 1 : S + 1, 0:C2].astype(BF))
        tips.append((total[0:1], total[S + 1 : S + 2]))
    io = iota2((16, C2), 0)
    ends = jnp.zeros((16, C2), F32)
    for corner, value in enumerate((tips[0][0], tips[1][0], tips[1][1], tips[0][1])):
        ends = jnp.where(io == corner, value, ends)
    pieces[4] = pack(jnp.concatenate([ends, ends], axis=0).astype(BF))
    second.to_x()
    piece_copies = near_copies(pieces, all_pieces, piece_sems, tile, ch, tiles)
    for copy in piece_copies:
        copy.start()
    loads[6].wait()

    def pick_weight(tap, carry):
        for part in range(2):
            input_half = ch if part == 0 else 1 - ch
            w = weight[tap, pl.ds(pl.multiple_of(input_half * C2, 64), C2)].astype(F32)
            out_weight[part, tap] = jnp.where(ch == 0, w[:, :C2], w[:, C2:]).astype(BF)
        return carry

    lax.fori_loop(0, 9, pick_weight, 0)
    second.to_z()
    first.to_gz()

    rows = S // 2

    def convolve_own(block, carry):
        total = None
        for a in range(3):
            for b in range(3):
                window = padded[b, pl.ds(block * rows + a, rows)].reshape(rows * S, C2)
                term = jnp.dot(window, out_weight[0, 3 * a + b], preferred_element_type=F32)
                total = term if total is None else total + term
        partial_out[pl.ds(block * rows, rows)] = total.reshape(rows, S, C2)
        return carry

    lax.fori_loop(0, 2, convolve_own, 0)
    first.to_gx()

    for copy in swap_b.second:
        copy.wait_recv()
    columns[0, 1 : S + 1] = unpack(packed_other[6, 4]).astype(F32)
    columns[1, 1 : S + 1] = unpack(packed_other[7, 0]).astype(F32)
    ends = unpack(packed_other[7, 1]).astype(F32)
    for corner in range(4):
        at = 0 if corner < 2 else S + 1
        columns[(0, 1, 1, 0)[corner], at : at + 1] = ends[corner : corner + 1]

    def shift_partner(row, carry):
        x = unpack(packed_other[row // 5, lax.rem(row, 5)]).astype(F32)
        spread_columns(
            shifted, row, slice(0, C2), x, columns[0, pl.ds(row, 1)], columns[1, pl.ds(row, 1)]
        )
        return carry

    lax.fori_loop(0, S + 2, shift_partner, 0, unroll=2)
    second.to_gz()
    first.to_gy()

    for copy in piece_copies:
        copy.wait_recv()
    for offset in OFFSETS:
        k = slot_of(-offset)
        source = wrap(tile - offset, tiles)
        for border in range(4):
            hit = edge_tiles[border, source] == tile
            slot = lookup(EDGE_TABLE, border, edge_turns[border, source])
            rev = slot // 4
            ii = iota2((S, 1), 0)
            target = jnp.where(rev == 1, S - 1 - ii, ii) + (slot - 4 * rev) * S
            hot = one_hot_rows(S, jnp.where(hit, target, -1), 4 * S)
            hits[0, k, border] = hot[:16]
            hits[1, k, border] = hot[16:]
        ii = iota2((16, 1), 0)
        target = jnp.full((16, 1), -1, jnp.int32)
        for corner in range(4):
            hit = corner_tiles[corner, source] == tile
            slot = lookup(CORNER_TABLE, corner, corner_turns[corner, source])
            cell = jnp.where(slot < 2, 0, 2 * S) + jnp.where((slot == 0) | (slot == 3), 0, S - 1)
            target = jnp.where((ii == corner) & hit, cell, target)
        hits[0, k, 4] = one_hot_rows(16, target, 4 * S)
        hits[1, k, 4] = jnp.zeros((16, 4 * S), BF)
    flat = all_pieces[...].reshape(8 * 5 * 16, C)
    parts = [
        lax.dot_general(hits[i].reshape(8 * 5 * 16, 4 * S), flat, TN, preferred_element_type=F32)
        for i in range(2)
    ]
    low = jnp.concatenate([parts[0][:, :128], parts[0][:, 256:320]], axis=1)
    high = jnp.concatenate([parts[1][:, 128:256], parts[1][:, 320:]], axis=1)
    sums[...] = (low + high).reshape(4, S, C2)
    second.to_gx()

    def add_sides(row, carry):
        io = iota2((S, C2), 0)
        x = interior[row + 1]
        x = x + jnp.where(io == 0, sums[3, pl.ds(row, 1)], 0.0)
        x = x + jnp.where(io == S - 1, sums[1, pl.ds(row, 1)], 0.0)
        x = x + jnp.where(row == 0, sums[0], 0.0)
        x = x + jnp.where(row == S - 1, sums[2], 0.0)
        grad_features[0, row] = x.astype(BF)
        return carry

    lax.fori_loop(0, S, add_sides, 0)
    first.to_pair()
    second.to_gy()

    def convolve_other(block, carry):
        total = partial_out[pl.ds(block * rows, rows)].reshape(rows * S, C2)
        for a in range(3):
            for b in range(3):
                window = shifted[b, pl.ds(block * rows + a, rows)].reshape(rows * S, C2)
                total = total + jnp.dot(window, out_weight[1, 3 * a + b], preferred_element_type=F32)
        output[0, pl.ds(block * rows, rows)] = total.reshape(rows, S, C2).astype(BF)
        return carry

    lax.fori_loop(0, 2, convolve_other, 0)
    second.to_pair()
    swap_a.finish_sends()
    swap_b.finish_sends()
    for copy in side_copies + piece_copies:
        copy.wait_send()
    first.finish()
    second.finish()


VSPEC = pl.BlockSpec(memory_space=VM)
ANY = pl.BlockSpec(memory_space=pl.ANY)
DMA = pltpu.SemaphoreType.DMA
SM = pltpu.SMEM
REDUCE_BUFS = [
    ((2, 4 * CHUNK), F32),
    ((4, CHUNK), F32),
    ((3, CHUNK), BF),
    ((3, CHUNK), BF),
    ((2, CHUNK // 2), F32),
    ((CHUNK // 2,), F32),
    ((7, UNIT), F32),
    ((7, UNIT), F32),
]
REDUCE_SEMS = [(2, 4), (2, 3), (2,), (2, 7), (2, 7), (2,), (2, 2, 3), (2, 2, 4)]


def reduce_scratch(width):
    return [VM(lead + (width,), kind) for lead, kind in REDUCE_BUFS] + [DMA(lead) for lead in REDUCE_SEMS]


def body(features, weight, cotangent, edge_tiles, edge_turns, corner_tiles, corner_turns):
    C2 = features.shape[3]
    C = 2 * C2
    shape = jax.ShapeDtypeStruct
    table = SM((4, 128), jnp.int32)
    output, grad_features, own_lanes, more_lanes = pl.pallas_call(
        lambda *refs: fused_kernel(1.0 / math.sqrt(128 * ROWS), *refs),
        name="fused",
        out_shape=(
            shape((1, S, S, C2), BF),
            shape((1, S, S, C2), BF),
            shape((2, 4, 2, 7, UNIT, 128), BF),
            shape((2, 4, 2, 7, UNIT, 256), BF),
        ),
        in_specs=[ANY] * 7,
        out_specs=(VSPEC,) * 4,
        scratch_shapes=[
            table, table, table, table,
            VM((S, S, C2), BF),
            VM((S, S, C2), BF),
            VM((9, C, C), BF),
            VM((9, C2, C), BF),
            VM((2, 9, C2, C2), BF),
            VM((2, S, C2), F32),
            VM((4, 16, C), BF),
            VM((8, 4, 16, C), BF),
            VM((8, 64, C), BF),
            VM((8, 64, C), BF),
            VM((2, 4, 64, C), BF),
            VM((3, S + 2, S, C2), BF),
            VM((2, 40, C2), F32),
            VM((3, S + 4, S, C), BF),
            VM((2, 48, C), F32),
            VM((S + 2, S, C2), F32),
            VM((5, 16, C), BF),
            VM((8, 5, 16, C), BF),
            VM((8, 5, 16, C), BF),
            VM((8, 5, 16, C), BF),
            VM((2, 4, 5, 16, C), BF),
            VM((3, S + 2, S, C2), BF),
            VM((S, S, C2), F32),
            VM((2, 8, 5, 16, 4 * S), BF),
            VM((4, S, C2), F32),
            DMA((8,)),
            DMA((2, 8)),
            DMA((4, 8)),
            DMA((4, 8)),
            DMA((2, 8)),
        ]
        + reduce_scratch(128)
        + reduce_scratch(256),
        compiler_params=pltpu.CompilerParams(
            vmem_limit_bytes=60 * 1024 * 1024, collective_id=0, has_side_effects=True
        ),
    )(
        edge_tiles.T, edge_turns.T, corner_tiles.T, corner_turns.T,
        features[0], cotangent[0], weight.reshape(9, C, C),
    )

    own_lanes = own_lanes.reshape(2, 4 * CHUNK, 128)[:, : 9 * (C2 // 2)]
    more_lanes = more_lanes.reshape(2, 4 * CHUNK, 256)[:, : 9 * (C2 // 2)]
    grad_weight = jnp.where(
        lax.axis_index("ch") == 0,
        jnp.concatenate([own_lanes, more_lanes], axis=2),
        jnp.concatenate([more_lanes, own_lanes], axis=2),
    )
    return (output, grad_features, grad_weight.astype(F32).reshape(3, 3, C2, C))


def solution(mesh):
    return jax.shard_map(
        body,
        mesh=mesh,
        in_specs=(
            P("tile", None, None, "ch"),
            P(),
            P("tile", None, None, "ch"),
            P(),
            P(),
            P(),
            P(),
        ),
        out_specs=(
            P("tile", None, None, "ch"),
            P("tile", None, None, "ch"),
            P(None, None, "ch", None),
        ),
        check_vma=False,
    )
```

time: 96.6 us -> 79.3 us (0.82)
  Pallas kernels: 84.4 us -> 72 us
  local copies, waits for them, and re-layouts: 10.7 us -> 3.93 us
  other arithmetic: 0 us -> 1.87 us
    pallas_call x1, Pallas kernels: 84.4 us -> 72 us  [body(): pl.pallas_call(lambda *refs: fused_kernel(1.0 / math.sqrt(128 * ROWS), *r...]
    unnamed x10 -> x6, local copies, waits for them, and re-layouts: 7.26 us -> 1.59 us
    convert_element_type x0 -> x1, other arithmetic: none -> 1.87 us  [body(): return (output, grad_features, grad_weight.astype(F32).reshape(3, 3, C2, C))]
    reshape x1 -> x0, local copies, waits for them, and re-layouts: 1.79 us -> none  [body(): flat.reshape(2, 9, C2 // 2, C).transpose(1, 0, 2, 3).astype(F32)]
where the time goes in v3:
time: 79.3 us; the launch traced here: 78.5 us
  Pallas kernels  72 us (91%)
  local copies, waits for them, and re-layouts  3.93 us (5%)
  other arithmetic  1.87 us (2%)
    pallas_call x1, Pallas kernels, body(): pl.pallas_call(lambda *refs: fused_kernel(1.0 / math.sqrt(128 * ROWS), *r...  72 us
    convert_element_type x1, other arithmetic, body(): return (output, grad_features, grad_weight.astype(F32).reshape(3, 3, C2, C))  1.87 us
    unnamed x6, local copies, waits for them, and re-layouts  1.59 us

profile of v3, /device:TPU:1, one launch (start us, length us, event | category | flops | bytes accessed | tf_op | source)
XLA Modules:
  0.0 78.5 jit_solution(9914691716815369633)
XLA Ops:
  0.6 72.0 %fused.1 = (bf16[1,32,32,192]{3,2,1,0:T(8,128)(2,1)}, bf16[1,32,32,192]{3,2,1,0:T(8,128)(2,1)}, bf16[2,4,2,7,16,128]{5,4,3,2,1,0:T(8,128)(2,1)}, bf16[2,4,2,7,16,256]{5,4,3,2,1,0:T(8,128)(2,1)}) custom-call(s32[4,128]{1,0:T(4,128)} %bitcast.18, s32[4,128]{1,0:T(4,128)} %bitcast.19, s32[4,128]{1,0:T(4,128)} %bitcast.20, s32[4,128]{1,0:T(4,128)} %bitcast.21, ...), custom_call_target="tpu_custom_call" | custom-call | tf_op jit(solution)/shard_map/fused/pallas_call | solution.py:656
  72.7 1.0 %slice.8 = bf16[2,864,128]{2,1,0:T(8,128)(2,1)S(1)} slice(bf16[2,896,128]{2,1,0:T(8,128)(2,1)} %bitcast.17), slice={[0:2], [0:864], [0:128]} | slice | bytes 884736 | tf_op jit(solution)/shard_map/slice | solution.py:710
  73.7 0.0 copy-start.1
  73.7 1.3 %slice.9 = bf16[2,864,256]{2,1,0:T(8,128)(2,1)S(1)} slice(bf16[2,896,256]{2,1,0:T(8,128)(2,1)} %bitcast.14), slice={[0:2], [0:864], [0:256]} | slice | bytes 1769472 | tf_op jit(solution)/shard_map/slice | solution.py:711
  75.0 0.0 copy-start
  75.0 1.9 %fusion = f32[3,3,192,384]{3,2,1,0:T(8,128)} fusion(bf16[3,3,192,256]{3,2,1,0:T(8,128)(2,1)S(1)} %bitcast.11, bf16[3,3,192,128]{3,2,1,0:T(8,128)(2,1)S(1)} %bitcast.13, pred[]{:T(512)S(6)} %eq.3), kind=kLoop, calls=%fused_computation.1 | loop fusion | flops 6635520 | bytes 3981313 | tf_op jit(solution)/shard_map/convert_element_type | solution.py:717
  76.9 0.0 copy-done.1
  76.9 0.8 %copy.12 = bf16[1,32,32,192]{3,2,1,0:T(8,128)(2,1)} copy(bf16[1,32,32,192]{3,2,1,0:T(8,128)(2,1)S(1)} %copy-done.1) | data formatting | bytes 786432
  77.7 0.0 copy-done
  77.7 0.8 %copy.13 = bf16[1,32,32,192]{3,2,1,0:T(8,128)(2,1)} copy(bf16[1,32,32,192]{3,2,1,0:T(8,128)(2,1)S(1)} %copy-done) | data formatting | bytes 786432
Async XLA Ops:
  73.7 3.2 %copy-start.1 = (bf16[1,32,32,192]{3,2,1,0:T(8,128)(2,1)S(1)}, bf16[1,32,32,192]{3,2,1,0:T(8,128)(2,1)}, u32[]{:S(2)}) copy-start(bf16[1,32,32,192]{3,2,1,0:T(8,128)(2,1)} %get-tuple-element.14) | copy-start | bytes 1179652
  75.0 2.7 %copy-start = (bf16[1,32,32,192]{3,2,1,0:T(8,128)(2,1)S(1)}, bf16[1,32,32,192]{3,2,1,0:T(8,128)(2,1)}, u32[]{:S(2)}) copy-start(bf16[1,32,32,192]{3,2,1,0:T(8,128)(2,1)} %get-tuple-element.15) | copy-start | bytes 1179652

commit v4 on v3

--- a/solution.py
+++ b/solution.py
@@ -171,139 +171,133 @@
 
 TN = (((0,), (0,)), ((), ()))
 NT = (((1,), (1,)), ((), ()))
-CHUNK = 14 * UNIT
+CHUNK = 7 * UNIT
 
 
 class Reduce:
-    def __init__(self, scale, bufs, sems, place):
-        self.grads, self.pair_in, self.y_out, self.y_in, self.acc, self.x_in, self.z_out, self.z_in, self.gathered = bufs
+    def __init__(self, scale, bufs, sems, place, z_first):
+        self.grads, self.pair_in, self.sent, self.got, self.unit_out, self.unit_in, self.gathered = bufs
         self.scale = scale
-        tile, ch, core, y, xl, z = self.place = place
-        self.near, _ = x_neighbours(tile, ch, xl)
+        tile, ch, core, y, xl, z = place
+        self.core = core
         self.pair = dev(tile + 1 - 2 * core, ch)
-        self.y_at = [lax.rem(y + 1 + j, 4) for j in range(3)]
-        self.y_peer = [dev(tile + 2 * (q - y), ch) for q in self.y_at]
-        self.z_at = [lax.rem(z + 1 + j, 8) for j in range(7)]
-        self.z_from = [lax.rem(z + 7 - j, 8) for j in range(7)]
-        self.z_peer = [dev(tile + 16 * (q - z), ch) for q in self.z_at]
-        self.order = self.y_at + [y]
-        pair_sems, y_sems, x_sems, z_sems, gz_sems, gx_sems, gy_sems, gp_sems = sems
-        self.pair_copies = []
-        for j, q in enumerate(self.order):
-            part = self.grads.at[1 - core, pl.ds(pl.multiple_of(q * CHUNK, CHUNK), CHUNK)]
-            self.pair_copies.append(
-                remote(part, self.pair_in.at[j], pair_sems.at[0, j], pair_sems.at[1, j], self.pair)
+        across = (2 * y + xl, lambda g: dev(tile + 2 * (g // 2 - y) + 8 * (lax.rem(g, 2) - xl), ch))
+        along = (z, lambda g: dev(tile + 16 * (g - z), ch))
+        (spot, outer), (unit, inner) = (along, across) if z_first else (across, along)
+        self.spot, self.unit = spot, unit
+        self.order = [lax.rem(spot + 1 + j, 8) for j in range(7)] + [spot]
+        self.unit_at = [lax.rem(unit + 1 + j, 8) for j in range(7)]
+        self.unit_from = [lax.rem(unit + 7 - j, 8) for j in range(7)]
+        self.outer_peers = [outer(g) for g in self.order[:7]]
+        self.inner_peers = [inner(g) for g in self.unit_at]
+        pair_sems, outer_sems, inner_sems, gather_sems, back_sems, last_sems = sems
+
+        def copy(src, dst, pool, j, where):
+            return remote(src, dst, pool.at[0, j], pool.at[1, j], where)
+
+        def rows(half, g):
+            return self.grads.at[half, pl.ds(pl.multiple_of(g * CHUNK, CHUNK), CHUNK)]
+
+        self.own = jnp.minimum(unit, 6)
+        mine = self.gathered.at[core, spot]
+        cell = mine.at[self.own]
+        seven = range(7)
+        self.pair_copies = [
+            copy(rows(1 - core, g), self.pair_in.at[j], pair_sems, j, self.pair)
+            for j, g in enumerate(self.order)
+        ]
+        self.copies = [
+            copy(self.sent.at[j], self.got.at[j], outer_sems, j, self.outer_peers[j]) for j in seven
+        ]
+        self.unit_copies = [
+            copy(
+                self.unit_out.at[jnp.minimum(self.unit_at[j], 6)], self.unit_in.at[j],
+                inner_sems, j, self.inner_peers[j],
             )
-        self.y_copies = [
-            remote(self.y_out.at[j], self.y_in.at[j], y_sems.at[0, j], y_sems.at[1, j], self.y_peer[j])
-            for j in range(3)
+            for j in seven
         ]
-        self.x_copy = remote(self.acc.at[1 - xl], self.x_in, x_sems.at[0], x_sems.at[1], self.near)
-        own = jnp.minimum(z, 6)
-        self.z_copies, self.gz_copies = [], []
-        for j in range(7):
-            part = self.z_out.at[jnp.minimum(self.z_at[j], 6)]
-            self.z_copies.append(remote(part, self.z_in.at[j], z_sems.at[0, j], z_sems.at[1, j], self.z_peer[j]))
-            spot = self.gathered.at[core, y, xl, own]
-            self.gz_copies.append(remote(spot, spot, gz_sems.at[0, j], gz_sems.at[1, j], self.z_peer[j]))
-        spot = self.gathered.at[core, y, xl]
-        self.gx_copy = remote(spot, spot, gx_sems.at[0], gx_sems.at[1], self.near)
-        self.gy_copies, self.gp_copies = [], []
-        for k in range(2):
-            half = xl if k == 0 else 1 - xl
-            spot = self.gathered.at[core, y, half]
-            for j in range(3):
-                self.gy_copies.append(
-                    remote(spot, spot, gy_sems.at[0, k, j], gy_sems.at[1, k, j], self.y_peer[j])
-                )
-            for j in range(4):
-                q = y if j == 0 else lax.rem(y + 4 - j, 4)
-                spot = self.gathered.at[core, q, half]
-                self.gp_copies.append(remote(spot, spot, gp_sems.at[0, k, j], gp_sems.at[1, k, j], self.pair))
+        self.gather = [copy(cell, cell, gather_sems, j, self.inner_peers[j]) for j in seven]
+        self.back = [copy(mine, mine, back_sems, j, self.outer_peers[j]) for j in seven]
+        self.last = []
+        for j in range(8):
+            block = self.gathered.at[core, spot if j == 0 else lax.rem(spot + 8 - j, 8)]
+            self.last.append(copy(block, block, last_sems, j, self.pair))
+
+    def own_rows(self, g):
+        return self.grads[self.core, pl.ds(pl.multiple_of(g * CHUNK, CHUNK), CHUNK)]
 
     def start(self):
         for copy in self.pair_copies:
             copy.start()
 
-    def to_y(self):
-        core = self.place[2]
-        for j in range(4):
+    def to_outer(self):
+        for j in range(7):
             self.pair_copies[j].wait_recv()
-            at = pl.multiple_of(self.order[j] * CHUNK, CHUNK)
-            total = self.grads[core, pl.ds(at, CHUNK)] + self.pair_in[j]
-            if j < 3:
-                self.y_out[j] = total.astype(BF)
-                self.y_copies[j].start()
-            else:
-                self.acc[...] = total.reshape(self.acc.shape)
-
-    def to_x(self):
-        for j in range(3):
-            self.y_copies[j].wait_recv()
-            self.acc[...] += self.y_in[j].astype(F32).reshape(self.acc.shape)
-        self.x_copy.start()
-
-    def to_z(self):
-        xl, z = self.place[4:]
-        self.x_copy.wait_recv()
-        self.z_out[...] = (self.acc[xl] + self.x_in[...]).reshape(self.z_out.shape)
+            self.sent[j] = (self.own_rows(self.order[j]) + self.pair_in[j]).astype(BF)
+            self.copies[j].start()
+
+    def to_inner(self):
+        self.pair_copies[7].wait_recv()
+        total = self.own_rows(self.spot) + self.pair_in[7]
         for j in range(7):
-            pl.when(self.z_at[j] != 7)(self.z_copies[j].start)
-
-    def to_gz(self):
-        tile, ch, core, y, xl, z = self.place
-
-        @pl.when(z != 7)
+            self.copies[j].wait_recv()
+            total = total + self.got[j].astype(F32)
+        self.unit_out[...] = total.reshape(self.unit_out.shape)
+        for j in range(7):
+            pl.when(self.unit_at[j] != 7)(self.unit_copies[j].start)
+
+    def to_gather(self):
+        @pl.when(self.unit != 7)
         def _():
-            own = jnp.minimum(z, 6)
-            total = self.z_out[own]
+            total = self.unit_out[self.own]
             for j in range(7):
-                self.z_copies[j].wait_recv()
-                total = total + self.z_in[j]
-            self.gathered[core, y, xl, own] = (total * self.scale).astype(BF)
-            for copy in self.gz_copies:
+                self.unit_copies[j].wait_recv()
+                total = total + self.unit_in[j]
+            self.gathered[self.core, self.spot, self.own] = (total * self.scale).astype(BF)
+            for copy in self.gather:
                 copy.start()
 
-    def to_gx(self):
+    def to_back(self):
         for j in range(7):
-            pl.when(self.z_from[j] != 7)(self.gz_copies[j].wait_recv)
-        self.gx_copy.start()
-        for copy in self.gy_copies[:3]:
+            pl.when(self.unit_from[j] != 7)(self.gather[j].wait_recv)
+        for copy in self.back:
             copy.start()
-        self.gp_copies[0].start()
-
-    def to_gy(self):
-        self.gx_copy.wait_recv()
-        for copy in self.gy_copies[3:]:
-            copy.start()
-        self.gp_copies[4].start()
+        self.last[0].start()
 
     def to_pair(self):
-        for k in range(2):
-            for j in range(3):
-                self.gy_copies[3 * k + j].wait_recv()
-                self.gp_copies[4 * k + j + 1].start()
+        for j in range(7):
+            self.back[j].wait_recv()
+            self.last[j + 1].start()
+
+    def store(self, out, half, lanes):
+        width = self.gathered.shape[4]
+        filled = 9 * (out.shape[1] // 4)
+        for g in range(8):
+            rows = min(CHUNK, filled - g * CHUNK)
+            block = self.gathered[half, g].astype(F32).reshape(CHUNK, width)
+            out[pl.ds(pl.multiple_of(half * filled + g * CHUNK, 16), rows), lanes] = block[:rows]
+
+    def finish_pair(self):
+        for copy in self.last:
+            copy.wait()
 
     def finish(self):
-        z = self.place[5]
-        for copy in self.gp_copies:
-            copy.wait()
-        for copy in self.pair_copies + self.y_copies + [self.x_copy, self.gx_copy] + self.gy_copies:
+        for copy in self.pair_copies + self.copies + self.back:
             copy.wait_send()
         for j in range(7):
-            pl.when(self.z_at[j] != 7)(self.z_copies[j].wait_send)
-            pl.when(z != 7)(self.gz_copies[j].wait_send)
+            pl.when(self.unit_at[j] != 7)(self.unit_copies[j].wait_send)
+            pl.when(self.unit != 7)(self.gather[j].wait_send)
 
 
 def fused_kernel(
     scale,
     edge_tiles_in, edge_turns_in, corner_tiles_in, corner_turns_in, feat_in, cot_in, weight_in,
-    output, grad_features, gathered_1, gathered_2,
+    output, grad_features, grad_weight,
     edge_tiles, edge_turns, corner_tiles, corner_turns,
     feat, cot, weight, rows_weight, out_weight,
     lines, sides, all_sides, cot_packed, cot_other, relay_a,
     padded, columns, cots, cot_columns, interior, pieces, all_pieces,
-    packed, packed_other, relay_b, shifted, partial_out, hits, sums,
+    packed, packed_other, relay_b, shifted, partial_out, hits, sums, turned,
     load_sems, side_sems, swap_a_sems, swap_b_sems, piece_sems,
     *streams,
 ):
@@ -314,11 +308,18 @@
     near, far = x_neighbours(tile, ch, xl)
     bufs = len(REDUCE_BUFS)
     sems = len(REDUCE_SEMS)
-    first = Reduce(scale, streams[:bufs] + (gathered_1,), streams[bufs : bufs + sems], place)
-    streams = streams[bufs + sems :]
-    second = Reduce(scale, streams[:bufs] + (gathered_2,), streams[bufs:], place)
+    first, second, third = [
+        Reduce(
+            scale,
+            streams[i * (bufs + sems) : i * (bufs + sems) + bufs],
+            streams[i * (bufs + sems) + bufs : (i + 1) * (bufs + sems)],
+            place,
+            i == 2,
+        )
+        for i in range(3)
+    ]
     greeted = [dev(wrap(tile + o, tiles), ch) for o in OFFSETS] + [near, far, first.pair]
-    greeted = greeted + first.y_peer + first.z_peer
+    greeted = greeted + first.outer_peers + first.inner_peers
     ready = pltpu.get_barrier_semaphore()
     for where in greeted:
         pl.semaphore_signal(ready, inc=1, device_id=where, device_id_type=MESH)
@@ -385,7 +386,7 @@
             cot_columns[1, pl.ds(row + 2, 1), lanes] = x[S - 1 : S]
             return carry
 
-        lax.fori_loop(0, S, shift, 0, unroll=4)
+        lax.fori_loop(0, S, shift, 0, unroll=8)
 
     def read_other(row):
         at = pl.multiple_of(lax.rem(row, 4) * 16, 16)
@@ -422,14 +423,50 @@
     padded[1, 1 : S + 1] = feat[...]
 
     def shift_features(row, carry):
-        packed[row // 5, lax.rem(row, 5)] = pack(padded[1, row])
         x = padded[1, row].astype(F32)
         spread_columns(
             padded, row, slice(0, C2), x, columns[0, pl.ds(row, 1)], columns[1, pl.ds(row, 1)]
         )
         return carry
 
-    lax.fori_loop(0, S + 2, shift_features, 0, unroll=2)
+    lax.fori_loop(0, S + 2, shift_features, 0, unroll=17)
+    for b in range(3):
+        turned[b * C2 : (b + 1) * C2] = padded[b].reshape((S + 2) * S, C2).T
+    filled = 9 * (C2 // 2)
+
+    def weight_grad(parts, lanes):
+        width = 128 * len(parts)
+        for a in range(3):
+            full = cots[1, 2 - a : 2 - a + S + 2, :, lanes].reshape((S + 2) * S, width)
+            result = jnp.dot(turned[...], full, preferred_element_type=F32)
+            for i, stream in enumerate(parts):
+                for half in range(2):
+                    low = max(half * filled, 3 * a * C2)
+                    high = min((half + 1) * filled, 3 * (a + 1) * C2)
+                    if low < high:
+                        stream.grads[half, low - half * filled : high - half * filled] = result[
+                            low - 3 * a * C2 : high - 3 * a * C2, 128 * i : 128 * (i + 1)
+                        ]
+        for stream in parts:
+            stream.grads[:, filled:] = jnp.zeros((2, 8 * CHUNK - filled, 128), F32)
+            stream.start()
+
+    lanes = [pl.ds(pl.multiple_of(at, 128), 128) for at in (256 * ch, 128 - 128 * ch, 256 - 128 * ch)]
+    weight_grad([first], lanes[0])
+    for copy in swap_a.second:
+        copy.wait_recv()
+    pl.when(ch == 0)(lambda: fill(read_other, slice(C2, C)))
+    pl.when(ch == 1)(lambda: fill(read_other, slice(0, C2)))
+    first.to_outer()
+    weight_grad([second, third], pl.ds(pl.multiple_of(128 - 128 * ch, 128), 256))
+    second.to_outer()
+    third.to_outer()
+
+    def pack_padded(row, carry):
+        packed[row // 5, lax.rem(row, 5)] = pack(padded[1, row])
+        return carry
+
+    lax.fori_loop(0, S + 2, pack_padded, 0, unroll=2)
     packed[6, 4] = pack(columns[0, 1 : S + 1].astype(BF))
     packed[7, 0] = pack(columns[1, 1 : S + 1].astype(BF))
     io = iota2((16, C2), 0)
@@ -443,40 +480,6 @@
     swap_b = Swap(packed, packed_other, relay_b, swap_b_sems, tile, ch, xl)
     swap_b.start()
 
-    def weight_grad(stream, at):
-        width = stream.grads.shape[2]
-        lanes = pl.ds(pl.multiple_of(at, 128), width)
-        block = C2 // 2
-
-        def one_tap(tap, carry):
-            a, b = tap // 3, lax.rem(tap, 3)
-            window = padded[b, pl.ds(a, S)].reshape(ROWS, C2)
-            full = cots[1, 2 : S + 2, :, lanes].reshape(ROWS, width)
-            part = lax.dot_general(window, full, TN, preferred_element_type=F32)
-            for i in range(2):
-                index = 2 * tap + i
-                half = index // 9
-                spot = pl.multiple_of((index - 9 * half) * block, 32)
-                stream.grads[half, pl.ds(spot, block)] = part[i * block : (i + 1) * block]
-            return carry
-
-        lax.fori_loop(0, 9, one_tap, 0)
-        filled = 9 * block
-        stream.grads[:, filled:] = jnp.zeros((2, stream.grads.shape[1] - filled, width), F32)
-
-    weight_grad(first, 256 * ch)
-    first.start()
-    first.to_y()
-    for copy in swap_a.second:
-        copy.wait_recv()
-    pl.when(ch == 0)(lambda: fill(read_other, slice(C2, C)))
-    pl.when(ch == 1)(lambda: fill(read_other, slice(0, C2)))
-    weight_grad(second, 128 - 128 * ch)
-    second.start()
-    swap_b.relay()
-    second.to_y()
-    first.to_x()
-
     loads[7].wait()
     half = (S + 2) // 2
 
@@ -491,7 +494,7 @@
         return carry
 
     lax.fori_loop(0, 2, feature_grad, 0)
-    first.to_z()
+    first.to_inner()
     pieces[0] = pack(interior[0].astype(BF))
     pieces[2] = pack(interior[S + 1].astype(BF))
     tips = []
@@ -509,7 +512,6 @@
     for corner, value in enumerate((tips[0][0], tips[1][0], tips[1][1], tips[0][1])):
         ends = jnp.where(io == corner, value, ends)
     pieces[4] = pack(jnp.concatenate([ends, ends], axis=0).astype(BF))
-    second.to_x()
     piece_copies = near_copies(pieces, all_pieces, piece_sems, tile, ch, tiles)
     for copy in piece_copies:
         copy.start()
@@ -523,8 +525,7 @@
         return carry
 
     lax.fori_loop(0, 9, pick_weight, 0)
-    second.to_z()
-    first.to_gz()
+    second.to_inner()
 
     rows = S // 2
 
@@ -539,30 +540,11 @@
         return carry
 
     lax.fori_loop(0, 2, convolve_own, 0)
-    first.to_gx()
-
-    for copy in swap_b.second:
-        copy.wait_recv()
-    columns[0, 1 : S + 1] = unpack(packed_other[6, 4]).astype(F32)
-    columns[1, 1 : S + 1] = unpack(packed_other[7, 0]).astype(F32)
-    ends = unpack(packed_other[7, 1]).astype(F32)
-    for corner in range(4):
-        at = 0 if corner < 2 else S + 1
-        columns[(0, 1, 1, 0)[corner], at : at + 1] = ends[corner : corner + 1]
-
-    def shift_partner(row, carry):
-        x = unpack(packed_other[row // 5, lax.rem(row, 5)]).astype(F32)
-        spread_columns(
-            shifted, row, slice(0, C2), x, columns[0, pl.ds(row, 1)], columns[1, pl.ds(row, 1)]
-        )
-        return carry
-
-    lax.fori_loop(0, S + 2, shift_partner, 0, unroll=2)
-    second.to_gz()
-    first.to_gy()
-
-    for copy in piece_copies:
-        copy.wait_recv()
+    first.to_gather()
+    swap_b.relay()
+    third.to_inner()
+    second.to_gather()
+
     for offset in OFFSETS:
         k = slot_of(-offset)
         source = wrap(tile - offset, tiles)
@@ -584,6 +566,33 @@
             target = jnp.where((ii == corner) & hit, cell, target)
         hits[0, k, 4] = one_hot_rows(16, target, 4 * S)
         hits[1, k, 4] = jnp.zeros((16, 4 * S), BF)
+
+    third.to_gather()
+    first.to_back()
+    second.to_back()
+    third.to_back()
+
+    for copy in swap_b.second:
+        copy.wait_recv()
+    columns[0, 1 : S + 1] = unpack(packed_other[6, 4]).astype(F32)
+    columns[1, 1 : S + 1] = unpack(packed_other[7, 0]).astype(F32)
+    ends = unpack(packed_other[7, 1]).astype(F32)
+    for corner in range(4):
+        at = 0 if corner < 2 else S + 1
+        columns[(0, 1, 1, 0)[corner], at : at + 1] = ends[corner : corner + 1]
+
+    def shift_partner(row, carry):
+        x = unpack(packed_other[row // 5, lax.rem(row, 5)]).astype(F32)
+        spread_columns(
+            shifted, row, slice(0, C2), x, columns[0, pl.ds(row, 1)], columns[1, pl.ds(row, 1)]
+        )
+        return carry
+
+    lax.fori_loop(0, S + 2, shift_partner, 0, unroll=2)
+    first.to_pair()
+    for copy in piece_copies:
+        copy.wait_recv()
+
     flat = all_pieces[...].reshape(8 * 5 * 16, C)
     parts = [
         lax.dot_general(hits[i].reshape(8 * 5 * 16, 4 * S), flat, TN, preferred_element_type=F32)
@@ -592,8 +601,6 @@
     low = jnp.concatenate([parts[0][:, :128], parts[0][:, 256:320]], axis=1)
     high = jnp.concatenate([parts[1][:, 128:256], parts[1][:, 320:]], axis=1)
     sums[...] = (low + high).reshape(4, S, C2)
-    second.to_gx()
-
     def add_sides(row, carry):
         io = iota2((S, C2), 0)
         x = interior[row + 1]
@@ -604,9 +611,7 @@
         grad_features[0, row] = x.astype(BF)
         return carry
 
-    lax.fori_loop(0, S, add_sides, 0)
-    first.to_pair()
-    second.to_gy()
+    lax.fori_loop(0, S, add_sides, 0, unroll=2)
 
     def convolve_other(block, carry):
         total = partial_out[pl.ds(block * rows, rows)].reshape(rows * S, C2)
@@ -619,29 +624,34 @@
 
     lax.fori_loop(0, 2, convolve_other, 0)
     second.to_pair()
+    third.to_pair()
+    for stream, spot in zip((first, second, third), lanes):
+        stream.store(grad_weight, core, spot)
+    for stream, spot in zip((first, second, third), lanes):
+        stream.finish_pair()
+        stream.store(grad_weight, 1 - core, spot)
     swap_a.finish_sends()
     swap_b.finish_sends()
     for copy in side_copies + piece_copies:
         copy.wait_send()
-    first.finish()
-    second.finish()
+    for stream in (first, second, third):
+        stream.finish()
 
 
 VSPEC = pl.BlockSpec(memory_space=VM)
-ANY = pl.BlockSpec(memory_space=pl.ANY)
+ANY = pl.BlockSpec(memory_space=pltpu.HBM)
 DMA = pltpu.SemaphoreType.DMA
 SM = pltpu.SMEM
 REDUCE_BUFS = [
-    ((2, 4 * CHUNK), F32),
-    ((4, CHUNK), F32),
-    ((3, CHUNK), BF),
-    ((3, CHUNK), BF),
-    ((2, CHUNK // 2), F32),
-    ((CHUNK // 2,), F32),
+    ((2, 8 * CHUNK), F32),
+    ((8, CHUNK), F32),
+    ((7, CHUNK), BF),
+    ((7, CHUNK), BF),
     ((7, UNIT), F32),
     ((7, UNIT), F32),
+    ((2, 8, 7, UNIT), BF),
 ]
-REDUCE_SEMS = [(2, 4), (2, 3), (2,), (2, 7), (2, 7), (2,), (2, 2, 3), (2, 2, 4)]
+REDUCE_SEMS = [(2, 8), (2, 7), (2, 7), (2, 7), (2, 7), (2, 8)]
 
 
 def reduce_scratch(width):
@@ -653,17 +663,16 @@
     C = 2 * C2
     shape = jax.ShapeDtypeStruct
     table = SM((4, 128), jnp.int32)
-    output, grad_features, own_lanes, more_lanes = pl.pallas_call(
+    output, grad_features, grad_weight = pl.pallas_call(
         lambda *refs: fused_kernel(1.0 / math.sqrt(128 * ROWS), *refs),
         name="fused",
         out_shape=(
             shape((1, S, S, C2), BF),
             shape((1, S, S, C2), BF),
-            shape((2, 4, 2, 7, UNIT, 128), BF),
-            shape((2, 4, 2, 7, UNIT, 256), BF),
+            shape((9 * C2, C), F32),
         ),
         in_specs=[ANY] * 7,
-        out_specs=(VSPEC,) * 4,
+        out_specs=(VSPEC,) * 3,
         scratch_shapes=[
             table, table, table, table,
             VM((S, S, C2), BF),
@@ -691,30 +700,23 @@
             VM((S, S, C2), F32),
             VM((2, 8, 5, 16, 4 * S), BF),
             VM((4, S, C2), F32),
+            VM((3 * C2, (S + 2) * S), BF),
             DMA((8,)),
             DMA((2, 8)),
             DMA((4, 8)),
             DMA((4, 8)),
             DMA((2, 8)),
         ]
-        + reduce_scratch(128)
-        + reduce_scratch(256),
+        + reduce_scratch(128) * 3,
         compiler_params=pltpu.CompilerParams(
-            vmem_limit_bytes=60 * 1024 * 1024, collective_id=0, has_side_effects=True
+            vmem_limit_bytes=44 * 1024 * 1024, collective_id=0, has_side_effects=True
         ),
     )(
-        edge_tiles.T, edge_turns.T, corner_tiles.T, corner_turns.T,
-        features[0], cotangent[0], weight.reshape(9, C, C),
+        *[pltpu.with_memory_space_constraint(x.T, pltpu.HBM) for x in (edge_tiles, edge_turns, corner_tiles, corner_turns)],
+        *[pltpu.with_memory_space_constraint(x, pltpu.HBM) for x in (features[0], cotangent[0], weight.reshape(9, C, C))],
     )
 
-    own_lanes = own_lanes.reshape(2, 4 * CHUNK, 128)[:, : 9 * (C2 // 2)]
-    more_lanes = more_lanes.reshape(2, 4 * CHUNK, 256)[:, : 9 * (C2 // 2)]
-    grad_weight = jnp.where(
-        lax.axis_index("ch") == 0,
-        jnp.concatenate([own_lanes, more_lanes], axis=2),
-        jnp.concatenate([more_lanes, own_lanes], axis=2),
-    )
-    return (output, grad_features, grad_weight.astype(F32).reshape(3, 3, C2, C))
+    return (output, grad_features, grad_weight.reshape(3, 3, C2, C))
 
 
 def solution(mesh):

time: 79.3 us -> 68.6 us (0.87)
  Pallas kernels: 72 us -> 64.8 us
  other arithmetic: 1.87 us -> 0 us
  local copies, waits for them, and re-layouts: 3.93 us -> 3.09 us
    pallas_call x1, Pallas kernels: 72 us -> 64.8 us  [body(): pl.pallas_call(lambda *refs: fused_kernel(1.0 / math.sqrt(128 * ROWS), *r...]
    slice x2 -> x0, local copies, waits for them, and re-layouts: 2.33 us -> none  [the longest x1 1.29 us: body(): more_lanes = more_lanes.reshape(2, 4 * CHUNK, 256)[:, :9 * (C2 // 2)]]
    convert_element_type x1 -> x0, other arithmetic: 1.87 us -> none  [body(): return (output, grad_features, grad_weight.astype(F32).reshape(3, 3, C2, C))]
    unnamed x6 -> x3, local copies, waits for them, and re-layouts: 1.59 us -> 3.09 us
where the time goes in v4:
time: 68.6 us; the launch traced here: 68.5 us
  Pallas kernels  64.8 us (94%)
  local copies, waits for them, and re-layouts  3.09 us (5%)
    pallas_call x1, Pallas kernels, body(): pl.pallas_call(lambda *refs: fused_kernel(1.0 / math.sqrt(128 * ROWS), *r...  64.8 us
    unnamed x3, local copies, waits for them, and re-layouts  3.09 us

profile of v4, /device:TPU:1, one launch (start us, length us, event | category | flops | bytes accessed | tf_op | source)
XLA Modules:
  0.0 68.5 jit_solution(8476066153455396898)
XLA Ops:
  0.6 64.8 %fused.1 = (bf16[1,32,32,192]{3,2,1,0:T(8,128)(2,1)S(1)}, bf16[1,32,32,192]{3,2,1,0:T(8,128)(2,1)S(1)}, f32[1728,384]{1,0:T(8,128)S(1)}) custom-call(s32[4,128]{1,0:T(4,128)} %bitcast.12, s32[4,128]{1,0:T(4,128)} %bitcast.13, s32[4,128]{1,0:T(4,128)} %bitcast.14, s32[4,128]{1,0:T(4,128)} %bitcast.15, bf16[32,32,192]{2,1,0:T(8,128)(2,1)} %bitcast.10, ...), custom_call_target="tpu_custom_call" | custom-call | tf_op jit(solution)/shard_map/fused/pallas_call | solution.py:666
  65.4 0.8 %copy.13 = bf16[1,32,32,192]{3,2,1,0:T(8,128)(2,1)} copy(bf16[1,32,32,192]{3,2,1,0:T(8,128)(2,1)S(1)} %get-tuple-element.12) | data formatting | bytes 786432
  66.2 0.8 %copy.14 = bf16[1,32,32,192]{3,2,1,0:T(8,128)(2,1)} copy(bf16[1,32,32,192]{3,2,1,0:T(8,128)(2,1)S(1)} %get-tuple-element.13) | data formatting | bytes 786432
  67.0 1.5 %copy.15 = f32[3,3,192,384]{3,2,1,0:T(8,128)} copy(f32[3,3,192,384]{3,2,1,0:T(8,128)S(1)} %bitcast.8) | data formatting | bytes 5308416

commit v5 on v4

--- a/solution.py
+++ b/solution.py
@@ -226,9 +226,10 @@
     def own_rows(self, g):
         return self.grads[self.core, pl.ds(pl.multiple_of(g * CHUNK, CHUNK), CHUNK)]
 
-    def start(self):
-        for copy in self.pair_copies:
-            copy.start()
+    def start(self, step, begin):
+        for g, copy in zip(self.order, self.pair_copies):
+            early = g <= 4 if begin == 0 else g >= 3
+            pl.when(early if step == 0 else jnp.logical_not(early))(copy.start)
 
     def to_outer(self):
         for j in range(7):
@@ -314,7 +315,7 @@
             streams[i * (bufs + sems) : i * (bufs + sems) + bufs],
             streams[i * (bufs + sems) + bufs : (i + 1) * (bufs + sems)],
             place,
-            i == 2,
+            False,
         )
         for i in range(3)
     ]
@@ -340,7 +341,7 @@
             )
         )
     ]
-    for load in loads:
+    for load in loads[:6]:
         load.start()
 
     loads[0].wait()
@@ -370,6 +371,8 @@
     side_copies = near_copies(sides, all_sides, side_sems, tile, ch, tiles)
     for copy in side_copies:
         copy.start()
+    for load in loads[6:]:
+        load.start()
 
     zero = jnp.zeros((S, C), BF)
     for part in range(3):
@@ -436,31 +439,47 @@
 
     def weight_grad(parts, lanes):
         width = 128 * len(parts)
-        for a in range(3):
-            full = cots[1, 2 - a : 2 - a + S + 2, :, lanes].reshape((S + 2) * S, width)
-            result = jnp.dot(turned[...], full, preferred_element_type=F32)
-            for i, stream in enumerate(parts):
-                for half in range(2):
-                    low = max(half * filled, 3 * a * C2)
-                    high = min((half + 1) * filled, 3 * (a + 1) * C2)
-                    if low < high:
-                        stream.grads[half, low - half * filled : high - half * filled] = result[
-                            low - 3 * a * C2 : high - 3 * a * C2, 128 * i : 128 * (i + 1)
-                        ]
         for stream in parts:
             stream.grads[:, filled:] = jnp.zeros((2, 8 * CHUNK - filled, 128), F32)
-            stream.start()
+
+        def products(order):
+            for step, a in enumerate(order):
+                full = cots[1, 2 - a : 2 - a + S + 2, :, lanes].reshape((S + 2) * S, width)
+                result = jnp.dot(turned[...], full, preferred_element_type=F32)
+                for i, stream in enumerate(parts):
+                    for half in range(2):
+                        low = max(half * filled, 3 * a * C2)
+                        high = min((half + 1) * filled, 3 * (a + 1) * C2)
+                        if low < high:
+                            stream.grads[half, low - half * filled : high - half * filled] = result[
+                                low - 3 * a * C2 : high - 3 * a * C2, 128 * i : 128 * (i + 1)
+                            ]
+                    if step < 2:
+                        stream.start(step, order[0])
+
+        pl.when(core == 1)(lambda: products((0, 1, 2)))
+        pl.when(core == 0)(lambda: products((2, 1, 0)))
 
     lanes = [pl.ds(pl.multiple_of(at, 128), 128) for at in (256 * ch, 128 - 128 * ch, 256 - 128 * ch)]
     weight_grad([first], lanes[0])
     for copy in swap_a.second:
         copy.wait_recv()
-    pl.when(ch == 0)(lambda: fill(read_other, slice(C2, C)))
-    pl.when(ch == 1)(lambda: fill(read_other, slice(0, C2)))
+
+    def place_other(lanes):
+        def one_row(row, carry):
+            cots[1, row + 2, :, lanes] = read_other(row)
+            return carry
+
+        lax.fori_loop(0, S, one_row, 0, unroll=8)
+
+    pl.when(ch == 0)(lambda: place_other(slice(C2, C)))
+    pl.when(ch == 1)(lambda: place_other(slice(0, C2)))
     first.to_outer()
     weight_grad([second, third], pl.ds(pl.multiple_of(128 - 128 * ch, 128), 256))
     second.to_outer()
     third.to_outer()
+    pl.when(ch == 0)(lambda: fill(read_other, slice(C2, C)))
+    pl.when(ch == 1)(lambda: fill(read_other, slice(0, C2)))
 
     def pack_padded(row, carry):
         packed[row // 5, lax.rem(row, 5)] = pack(padded[1, row])
@@ -480,6 +499,7 @@
     swap_b = Swap(packed, packed_other, relay_b, swap_b_sems, tile, ch, xl)
     swap_b.start()
 
+    first.to_inner()
     loads[7].wait()
     half = (S + 2) // 2
 
@@ -494,7 +514,6 @@
         return carry
 
     lax.fori_loop(0, 2, feature_grad, 0)
-    first.to_inner()
     pieces[0] = pack(interior[0].astype(BF))
     pieces[2] = pack(interior[S + 1].astype(BF))
     tips = []
@@ -512,9 +531,6 @@
     for corner, value in enumerate((tips[0][0], tips[1][0], tips[1][1], tips[0][1])):
         ends = jnp.where(io == corner, value, ends)
     pieces[4] = pack(jnp.concatenate([ends, ends], axis=0).astype(BF))
-    piece_copies = near_copies(pieces, all_pieces, piece_sems, tile, ch, tiles)
-    for copy in piece_copies:
-        copy.start()
     loads[6].wait()
 
     def pick_weight(tap, carry):
@@ -526,6 +542,12 @@
 
     lax.fori_loop(0, 9, pick_weight, 0)
     second.to_inner()
+    third.to_inner()
+    piece_copies = near_copies(pieces, all_pieces, piece_sems, tile, ch, tiles)
+    for copy in piece_copies:
+        copy.start()
+
+    first.to_gather()
 
     rows = S // 2
 
@@ -540,10 +562,9 @@
         return carry
 
     lax.fori_loop(0, 2, convolve_own, 0)
-    first.to_gather()
+    second.to_gather()
+    third.to_gather()
     swap_b.relay()
-    third.to_inner()
-    second.to_gather()
 
     for offset in OFFSETS:
         k = slot_of(-offset)
@@ -567,7 +588,6 @@
         hits[0, k, 4] = one_hot_rows(16, target, 4 * S)
         hits[1, k, 4] = jnp.zeros((16, 4 * S), BF)
 
-    third.to_gather()
     first.to_back()
     second.to_back()
     third.to_back()
@@ -636,6 +656,17 @@
         copy.wait_send()
     for stream in (first, second, third):
         stream.finish()
+
+
+def publish_kernel(a, b, c, a_out, b_out, c_out, sems):
+    copies = [
+        pltpu.make_async_copy(src, dst, sems.at[i])
+        for i, (src, dst) in enumerate(((c, c_out), (a, a_out), (b, b_out)))
+    ]
+    for copy in copies:
+        copy.start()
+    for copy in copies:
+        copy.wait()
 
 
 VSPEC = pl.BlockSpec(memory_space=VM)
@@ -716,6 +747,15 @@
         *[pltpu.with_memory_space_constraint(x, pltpu.HBM) for x in (features[0], cotangent[0], weight.reshape(9, C, C))],
     )
 
+    output, grad_features, grad_weight = pl.pallas_call(
+        publish_kernel,
+        name="publish",
+        out_shape=(shape((1, S, S, C2), BF), shape((1, S, S, C2), BF), shape((9 * C2, C), F32)),
+        in_specs=[pl.BlockSpec(memory_space=pl.ANY)] * 3,
+        out_specs=(ANY,) * 3,
+        scratch_shapes=[DMA((3,))],
+        compiler_params=pltpu.CompilerParams(vmem_limit_bytes=1024 * 1024),
+    )(output, grad_features, grad_weight)
     return (output, grad_features, grad_weight.reshape(3, 3, C2, C))
 
 

time: 68.6 us -> 65.4 us (0.953)
  local copies, waits for them, and re-layouts: 3.09 us -> 0 us
    unnamed x3 -> x0, local copies, waits for them, and re-layouts: 3.09 us -> none
    pallas_call x1, Pallas kernels: 64.8 us -> 62.6 us  [body(): pl.pallas_call(lambda *refs: fused_kernel(1.0 / math.sqrt(128 * ROWS), *r...]
    pallas_call x0 -> x1, Pallas kernels: none -> 1.87 us  [body(): pl.pallas_call(publish_kernel, name='publish', out_shape=(shape((1, S, S,...]
where the time goes in v5:
time: 65.4 us; the launch traced here: 65.3 us
  Pallas kernels  64.5 us (99%)
  between operations  0.8 us (1%)
    pallas_call x1, Pallas kernels, body(): pl.pallas_call(lambda *refs: fused_kernel(1.0 / math.sqrt(128 * ROWS), *r...  62.6 us
    pallas_call x1, Pallas kernels, body(): pl.pallas_call(publish_kernel, name='publish', out_shape=(shape((1, S, S,...  1.87 us

profile of v5, /device:TPU:1, one launch (start us, length us, event | category | flops | bytes accessed | tf_op | source)
XLA Modules:
  0.0 65.3 jit_solution(10952903145346759306)
XLA Ops:
  0.6 62.6 %fused.1 = (bf16[1,32,32,192]{3,2,1,0:T(8,128)(2,1)S(1)}, bf16[1,32,32,192]{3,2,1,0:T(8,128)(2,1)S(1)}, f32[1728,384]{1,0:T(8,128)S(1)}) custom-call(s32[4,128]{1,0:T(4,128)} %bitcast.11, s32[4,128]{1,0:T(4,128)} %bitcast.12, s32[4,128]{1,0:T(4,128)} %bitcast.13, s32[4,128]{1,0:T(4,128)} %bitcast.14, bf16[32,32,192]{2,1,0:T(8,128)(2,1)} %bitcast.9, ...), custom_call_target="tpu_custom_call" | custom-call | tf_op jit(solution)/shard_map/fused/pallas_call | solution.py:697
  63.3 1.9 %publish.1 = (bf16[1,32,32,192]{3,2,1,0:T(8,128)(2,1)}, bf16[1,32,32,192]{3,2,1,0:T(8,128)(2,1)}, f32[1728,384]{1,0:T(8,128)}) custom-call(bf16[1,32,32,192]{3,2,1,0:T(8,128)(2,1)S(1)} %get-tuple-element.9.a, bf16[1,32,32,192]{3,2,1,0:T(8,128)(2,1)S(1)} %get-tuple-element.10.b, f32[1728,384]{1,0:T(8,128)S(1)} %get-tuple-element.11.c), custom_call_target="tpu_custom_call" | custom-call | tf_op jit(solution)/shard_map/publish/pallas_call | solution.py:750

commit v6 on v5

--- a/solution.py
+++ b/solution.py
@@ -117,8 +117,8 @@
         for copy in self.first:
             copy.start()
 
-    def relay(self):
-        for one, two in zip(self.first, self.second):
+    def relay(self, start=0, stop=None):
+        for one, two in zip(self.first[start:stop], self.second[start:stop]):
             one.wait_recv()
             two.start()
 
@@ -175,7 +175,7 @@
 
 
 class Reduce:
-    def __init__(self, scale, bufs, sems, place, z_first):
+    def __init__(self, scale, bufs, sems, place):
         self.grads, self.pair_in, self.sent, self.got, self.unit_out, self.unit_in, self.gathered = bufs
         self.scale = scale
         tile, ch, core, y, xl, z = place
@@ -183,7 +183,7 @@
         self.pair = dev(tile + 1 - 2 * core, ch)
         across = (2 * y + xl, lambda g: dev(tile + 2 * (g // 2 - y) + 8 * (lax.rem(g, 2) - xl), ch))
         along = (z, lambda g: dev(tile + 16 * (g - z), ch))
-        (spot, outer), (unit, inner) = (along, across) if z_first else (across, along)
+        (spot, outer), (unit, inner) = across, along
         self.spot, self.unit = spot, unit
         self.order = [lax.rem(spot + 1 + j, 8) for j in range(7)] + [spot]
         self.unit_at = [lax.rem(unit + 1 + j, 8) for j in range(7)]
@@ -217,10 +217,18 @@
             for j in seven
         ]
         self.gather = [copy(cell, cell, gather_sems, j, self.inner_peers[j]) for j in seven]
-        self.back = [copy(mine, mine, back_sems, j, self.outer_peers[j]) for j in seven]
+        near, _ = x_neighbours(tile, ch, xl)
+        column = [dev(tile + 2 * (lax.rem(y + 1 + j, 4) - y), ch) for j in range(3)]
+        beside = self.gathered.at[core, 2 * y + 1 - xl]
+        self.back = [copy(mine, mine, back_sems, 0, near)]
+        self.back += [copy(mine, mine, back_sems, 1 + j, column[j]) for j in range(3)]
+        self.back += [copy(beside, beside, back_sems, 4 + j, column[j]) for j in range(3)]
+        got = [2 * y + 1 - xl]
+        for other in (xl, 1 - xl):
+            got += [2 * lax.rem(y + 3 - j, 4) + other for j in range(3)]
         self.last = []
-        for j in range(8):
-            block = self.gathered.at[core, spot if j == 0 else lax.rem(spot + 8 - j, 8)]
+        for j, g in enumerate([spot] + got):
+            block = self.gathered.at[core, g]
             self.last.append(copy(block, block, last_sems, j, self.pair))
 
     def own_rows(self, g):
@@ -261,12 +269,18 @@
     def to_back(self):
         for j in range(7):
             pl.when(self.unit_from[j] != 7)(self.gather[j].wait_recv)
-        for copy in self.back:
+        for copy in self.back[:4]:
             copy.start()
         self.last[0].start()
 
+    def pass_back(self):
+        self.back[0].wait_recv()
+        for copy in self.back[4:]:
+            copy.start()
+        self.last[1].start()
+
     def to_pair(self):
-        for j in range(7):
+        for j in range(1, 7):
             self.back[j].wait_recv()
             self.last[j + 1].start()
 
@@ -315,7 +329,6 @@
             streams[i * (bufs + sems) : i * (bufs + sems) + bufs],
             streams[i * (bufs + sems) + bufs : (i + 1) * (bufs + sems)],
             place,
-            False,
         )
         for i in range(3)
     ]
@@ -478,8 +491,6 @@
     weight_grad([second, third], pl.ds(pl.multiple_of(128 - 128 * ch, 128), 256))
     second.to_outer()
     third.to_outer()
-    pl.when(ch == 0)(lambda: fill(read_other, slice(C2, C)))
-    pl.when(ch == 1)(lambda: fill(read_other, slice(0, C2)))
 
     def pack_padded(row, carry):
         packed[row // 5, lax.rem(row, 5)] = pack(padded[1, row])
@@ -498,6 +509,9 @@
         packed[7, i] = jnp.zeros((16, C), BF)
     swap_b = Swap(packed, packed_other, relay_b, swap_b_sems, tile, ch, xl)
     swap_b.start()
+
+    pl.when(ch == 0)(lambda: fill(read_other, slice(C2, C)))
+    pl.when(ch == 1)(lambda: fill(read_other, slice(0, C2)))
 
     first.to_inner()
     loads[7].wait()
@@ -562,9 +576,10 @@
         return carry
 
     lax.fori_loop(0, 2, convolve_own, 0)
+    swap_b.relay(0, 4)
     second.to_gather()
+    swap_b.relay(4)
     third.to_gather()
-    swap_b.relay()
 
     for offset in OFFSETS:
         k = slot_of(-offset)
@@ -591,6 +606,9 @@
     first.to_back()
     second.to_back()
     third.to_back()
+    first.pass_back()
+    second.pass_back()
+    third.pass_back()
 
     for copy in swap_b.second:
         copy.wait_recv()
@@ -609,7 +627,6 @@
         return carry
 
     lax.fori_loop(0, S + 2, shift_partner, 0, unroll=2)
-    first.to_pair()
     for copy in piece_copies:
         copy.wait_recv()
 
@@ -643,6 +660,7 @@
         return carry
 
     lax.fori_loop(0, 2, convolve_other, 0)
+    first.to_pair()
     second.to_pair()
     third.to_pair()
     for stream, spot in zip((first, second, third), lanes):

time: 65.4 us -> 62.4 us (0.954)
  Pallas kernels: 64.5 us -> 61.5 us
    pallas_call x1, Pallas kernels: 62.6 us -> 59.7 us  [body(): pl.pallas_call(lambda *refs: fused_kernel(1.0 / math.sqrt(128 * ROWS), *r...]
where the time goes in v6:
time: 62.4 us; the launch traced here: 62.3 us
  Pallas kernels  61.5 us (99%)
  between operations  0.8 us (1%)
    pallas_call x1, Pallas kernels, body(): pl.pallas_call(lambda *refs: fused_kernel(1.0 / math.sqrt(128 * ROWS), *r...  59.7 us
    pallas_call x1, Pallas kernels, body(): pl.pallas_call(publish_kernel, name='publish', out_shape=(shape((1, S, S,...  1.87 us

profile of v6, /device:TPU:1, one launch (start us, length us, event | category | flops | bytes accessed | tf_op | source)
XLA Modules:
  0.0 62.3 jit_solution(6535726871431376531)
XLA Ops:
  0.6 59.7 %fused.1 = (bf16[1,32,32,192]{3,2,1,0:T(8,128)(2,1)S(1)}, bf16[1,32,32,192]{3,2,1,0:T(8,128)(2,1)S(1)}, f32[1728,384]{1,0:T(8,128)S(1)}) custom-call(s32[4,128]{1,0:T(4,128)} %bitcast.11, s32[4,128]{1,0:T(4,128)} %bitcast.12, s32[4,128]{1,0:T(4,128)} %bitcast.13, s32[4,128]{1,0:T(4,128)} %bitcast.14, bf16[32,32,192]{2,1,0:T(8,128)(2,1)} %bitcast.9, ...), custom_call_target="tpu_custom_call" | custom-call | tf_op jit(solution)/shard_map/fused/pallas_call | solution.py:715
  60.3 1.9 %publish.1 = (bf16[1,32,32,192]{3,2,1,0:T(8,128)(2,1)}, bf16[1,32,32,192]{3,2,1,0:T(8,128)(2,1)}, f32[1728,384]{1,0:T(8,128)}) custom-call(bf16[1,32,32,192]{3,2,1,0:T(8,128)(2,1)S(1)} %get-tuple-element.9.a, bf16[1,32,32,192]{3,2,1,0:T(8,128)(2,1)S(1)} %get-tuple-element.10.b, f32[1728,384]{1,0:T(8,128)S(1)} %get-tuple-element.11.c), custom_call_target="tpu_custom_call" | custom-call | tf_op jit(solution)/shard_map/publish/pallas_call | solution.py:768

commit v7 on v6

--- a/solution.py
+++ b/solution.py
@@ -202,10 +202,11 @@
         mine = self.gathered.at[core, spot]
         cell = mine.at[self.own]
         seven = range(7)
-        self.pair_copies = [
-            copy(rows(1 - core, g), self.pair_in.at[j], pair_sems, j, self.pair)
-            for j, g in enumerate(self.order)
-        ]
+        def pair_copy(g):
+            return copy(rows(1 - core, g), self.pair_in.at[g], pair_sems, g, self.pair)
+
+        self.pair_starts = [pair_copy(g) for g in range(8)]
+        self.pair_copies = [pair_copy(g) for g in self.order]
         self.copies = [
             copy(self.sent.at[j], self.got.at[j], outer_sems, j, self.outer_peers[j]) for j in seven
         ]
@@ -235,19 +236,20 @@
         return self.grads[self.core, pl.ds(pl.multiple_of(g * CHUNK, CHUNK), CHUNK)]
 
     def start(self, step, begin):
-        for g, copy in zip(self.order, self.pair_copies):
+        for g, copy in enumerate(self.pair_starts):
             early = g <= 4 if begin == 0 else g >= 3
-            pl.when(early if step == 0 else jnp.logical_not(early))(copy.start)
+            if early == (step == 0):
+                copy.start()
 
     def to_outer(self):
         for j in range(7):
             self.pair_copies[j].wait_recv()
-            self.sent[j] = (self.own_rows(self.order[j]) + self.pair_in[j]).astype(BF)
+            self.sent[j] = (self.own_rows(self.order[j]) + self.pair_in[self.order[j]]).astype(BF)
             self.copies[j].start()
 
     def to_inner(self):
         self.pair_copies[7].wait_recv()
-        total = self.own_rows(self.spot) + self.pair_in[7]
+        total = self.own_rows(self.spot) + self.pair_in[self.spot]
         for j in range(7):
             self.copies[j].wait_recv()
             total = total + self.got[j].astype(F32)
@@ -545,6 +547,13 @@
     for corner, value in enumerate((tips[0][0], tips[1][0], tips[1][1], tips[0][1])):
         ends = jnp.where(io == corner, value, ends)
     pieces[4] = pack(jnp.concatenate([ends, ends], axis=0).astype(BF))
+    second.to_inner()
+    third.to_inner()
+    piece_copies = near_copies(pieces, all_pieces, piece_sems, tile, ch, tiles)
+    for copy in piece_copies:
+        copy.start()
+
+    first.to_gather()
     loads[6].wait()
 
     def pick_weight(tap, carry):
@@ -555,13 +564,7 @@
         return carry
 
     lax.fori_loop(0, 9, pick_weight, 0)
-    second.to_inner()
-    third.to_inner()
-    piece_copies = near_copies(pieces, all_pieces, piece_sems, tile, ch, tiles)
-    for copy in piece_copies:
-        copy.start()
-
-    first.to_gather()
+    swap_b.relay(0, 4)
 
     rows = S // 2
 
@@ -576,9 +579,9 @@
         return carry
 
     lax.fori_loop(0, 2, convolve_own, 0)
-    swap_b.relay(0, 4)
+    swap_b.relay(4, 6)
     second.to_gather()
-    swap_b.relay(4)
+    swap_b.relay(6)
     third.to_gather()
 
     for offset in OFFSETS:
@@ -679,7 +682,10 @@
 def publish_kernel(a, b, c, a_out, b_out, c_out, sems):
     copies = [
         pltpu.make_async_copy(src, dst, sems.at[i])
-        for i, (src, dst) in enumerate(((c, c_out), (a, a_out), (b, b_out)))
+        for i, (src, dst) in enumerate(
+            [(c.at[pl.ds(k * 432, 432)], c_out.at[pl.ds(k * 432, 432)]) for k in range(4)]
+            + [(a, a_out), (b, b_out)]
+        )
     ]
     for copy in copies:
         copy.start()
@@ -771,7 +777,7 @@
         out_shape=(shape((1, S, S, C2), BF), shape((1, S, S, C2), BF), shape((9 * C2, C), F32)),
         in_specs=[pl.BlockSpec(memory_space=pl.ANY)] * 3,
         out_specs=(ANY,) * 3,
-        scratch_shapes=[DMA((3,))],
+        scratch_shapes=[DMA((6,))],
         compiler_params=pltpu.CompilerParams(vmem_limit_bytes=1024 * 1024),
     )(output, grad_features, grad_weight)
     return (output, grad_features, grad_weight.reshape(3, 3, C2, C))

time: 62.4 us -> 64.7 us (1.037)
  Pallas kernels: 61.5 us -> 63.8 us
    pallas_call x1, Pallas kernels: 59.7 us -> 61.9 us  [body(): pl.pallas_call(lambda *refs: fused_kernel(1.0 / math.sqrt(128 * ROWS), *r...]
where the time goes in v7:
time: 64.7 us; the launch traced here: 64.6 us
  Pallas kernels  63.8 us (99%)
  between operations  0.8 us (1%)
    pallas_call x1, Pallas kernels, body(): pl.pallas_call(lambda *refs: fused_kernel(1.0 / math.sqrt(128 * ROWS), *r...  61.9 us
    pallas_call x1, Pallas kernels, body(): pl.pallas_call(publish_kernel, name='publish', out_shape=(shape((1, S, S,...  1.89 us

profile of v7, /device:TPU:1, one launch (start us, length us, event | category | flops | bytes accessed | tf_op | source)
XLA Modules:
  0.0 64.6 jit_solution(9306027723304958465)
XLA Ops:
  0.6 61.9 %fused.1 = (bf16[1,32,32,192]{3,2,1,0:T(8,128)(2,1)S(1)}, bf16[1,32,32,192]{3,2,1,0:T(8,128)(2,1)S(1)}, f32[1728,384]{1,0:T(8,128)S(1)}) custom-call(s32[4,128]{1,0:T(4,128)} %bitcast.11, s32[4,128]{1,0:T(4,128)} %bitcast.12, s32[4,128]{1,0:T(4,128)} %bitcast.13, s32[4,128]{1,0:T(4,128)} %bitcast.14, bf16[32,32,192]{2,1,0:T(8,128)(2,1)} %bitcast.9, ...), custom_call_target="tpu_custom_call" | custom-call | tf_op jit(solution)/shard_map/fused/pallas_call | solution.py:721
  62.6 1.9 %publish.1 = (bf16[1,32,32,192]{3,2,1,0:T(8,128)(2,1)}, bf16[1,32,32,192]{3,2,1,0:T(8,128)(2,1)}, f32[1728,384]{1,0:T(8,128)}) custom-call(bf16[1,32,32,192]{3,2,1,0:T(8,128)(2,1)S(1)} %get-tuple-element.9.a, bf16[1,32,32,192]{3,2,1,0:T(8,128)(2,1)S(1)} %get-tuple-element.10.b, f32[1728,384]{1,0:T(8,128)S(1)} %get-tuple-element.11.c), custom_call_target="tpu_custom_call" | custom-call | tf_op jit(solution)/shard_map/publish/pallas_call | solution.py:774

commit v8 on v7

--- a/solution.py
+++ b/solution.py
@@ -547,6 +547,16 @@
     for corner, value in enumerate((tips[0][0], tips[1][0], tips[1][1], tips[0][1])):
         ends = jnp.where(io == corner, value, ends)
     pieces[4] = pack(jnp.concatenate([ends, ends], axis=0).astype(BF))
+    loads[6].wait()
+
+    def pick_weight(tap, carry):
+        for part in range(2):
+            input_half = ch if part == 0 else 1 - ch
+            w = weight[tap, pl.ds(pl.multiple_of(input_half * C2, 64), C2)].astype(F32)
+            out_weight[part, tap] = jnp.where(ch == 0, w[:, :C2], w[:, C2:]).astype(BF)
+        return carry
+
+    lax.fori_loop(0, 9, pick_weight, 0)
     second.to_inner()
     third.to_inner()
     piece_copies = near_copies(pieces, all_pieces, piece_sems, tile, ch, tiles)
@@ -554,16 +564,6 @@
         copy.start()
 
     first.to_gather()
-    loads[6].wait()
-
-    def pick_weight(tap, carry):
-        for part in range(2):
-            input_half = ch if part == 0 else 1 - ch
-            w = weight[tap, pl.ds(pl.multiple_of(input_half * C2, 64), C2)].astype(F32)
-            out_weight[part, tap] = jnp.where(ch == 0, w[:, :C2], w[:, C2:]).astype(BF)
-        return carry
-
-    lax.fori_loop(0, 9, pick_weight, 0)
     swap_b.relay(0, 4)
 
     rows = S // 2

time: 64.7 us -> 62.7 us (0.969)
  Pallas kernels: 63.8 us -> 61.8 us
    pallas_call x1, Pallas kernels: 61.9 us -> 59.9 us  [body(): pl.pallas_call(lambda *refs: fused_kernel(1.0 / math.sqrt(128 * ROWS), *r...]
where the time goes in v8:
time: 62.7 us; the launch traced here: 62.6 us
  Pallas kernels  61.8 us (99%)
  between operations  0.8 us (1%)
    pallas_call x1, Pallas kernels, body(): pl.pallas_call(lambda *refs: fused_kernel(1.0 / math.sqrt(128 * ROWS), *r...  59.9 us
    pallas_call x1, Pallas kernels, body(): pl.pallas_call(publish_kernel, name='publish', out_shape=(shape((1, S, S,...  1.89 us

profile of v8, /device:TPU:1, one launch (start us, length us, event | category | flops | bytes accessed | tf_op | source)
XLA Modules:
  0.0 62.6 jit_solution(14163003922066277566)
XLA Ops:
  0.6 59.9 %fused.1 = (bf16[1,32,32,192]{3,2,1,0:T(8,128)(2,1)S(1)}, bf16[1,32,32,192]{3,2,1,0:T(8,128)(2,1)S(1)}, f32[1728,384]{1,0:T(8,128)S(1)}) custom-call(s32[4,128]{1,0:T(4,128)} %bitcast.11, s32[4,128]{1,0:T(4,128)} %bitcast.12, s32[4,128]{1,0:T(4,128)} %bitcast.13, s32[4,128]{1,0:T(4,128)} %bitcast.14, bf16[32,32,192]{2,1,0:T(8,128)(2,1)} %bitcast.9, ...), custom_call_target="tpu_custom_call" | custom-call | tf_op jit(solution)/shard_map/fused/pallas_call | solution.py:721
  60.6 1.9 %publish.1 = (bf16[1,32,32,192]{3,2,1,0:T(8,128)(2,1)}, bf16[1,32,32,192]{3,2,1,0:T(8,128)(2,1)}, f32[1728,384]{1,0:T(8,128)}) custom-call(bf16[1,32,32,192]{3,2,1,0:T(8,128)(2,1)S(1)} %get-tuple-element.9.a, bf16[1,32,32,192]{3,2,1,0:T(8,128)(2,1)S(1)} %get-tuple-element.10.b, f32[1728,384]{1,0:T(8,128)S(1)} %get-tuple-element.11.c), custom_call_target="tpu_custom_call" | custom-call | tf_op jit(solution)/shard_map/publish/pallas_call | solution.py:774
